TPU v7x, 32 devices: a whole 2x2x4 slice. The times are simulated.
32 devices in a mesh: expert: 2 (over x), shard: 16 (over z, y, core).
Axes of the slice: x: 2, y: 2, z: 4, core: 2. Of those that a mesh axis runs over, the one named last changes fastest.
Arguments:
- tokens: bfloat16 [16, 512, 768], P('shard', 'expert'), may hold values from -32 to 32
- segment_ids: int32 [16, 512], P('shard'), may hold values from 0 to 3, never falling along the last dimension, each value on 1 to 256 neighbouring positions
- routes: int32 [16, 512, 2], P('shard', 'expert'), may hold values from 0 to 11, as said below
- earlier_logits: float32 [16, 512, 12], P('shard', 'expert'), may hold values from -3 to 3
- out_cotangent: bfloat16 [16, 512, 768], P('shard', 'expert'), may hold values from -6 to 6
- query_weight: bfloat16 [768, 768], P('shard'), may hold values from -0.3125 to 0.3125
- key_weight: bfloat16 [768, 768], P('shard'), may hold values from -0.3125 to 0.3125
- value_weight: bfloat16 [768, 768], P('shard'), may hold values from -0.21875 to 0.21875
- output_weight: bfloat16 [768, 768], P('shard'), may hold values from -0.875 to 0.875
- router_weight: bfloat16 [768, 12], P('shard'), may hold values from -0.109375 to 0.109375
- const_vectors: bfloat16 [768, 2], P('shard'), may hold values from -4 to 4
- attn_gain: bfloat16 [768], P('shard'), may hold values from 0.5 to 1.5
- moe_gain: bfloat16 [768], P('shard'), may hold values from 0.5 to 1.5
- gate_weight: bfloat16 [8, 768, 2048], P('expert', 'shard'), may hold values from -0.21875 to 0.21875
- up_weight: bfloat16 [8, 768, 2048], P('expert', 'shard'), may hold values from -0.21875 to 0.21875
- down_weight: bfloat16 [8, 2048, 768], P('expert', 'shard'), may hold values from -0.125 to 0.125
Outputs:
- layer_out: bfloat16 [16, 512, 768], P('shard', 'expert')
- tokens_grad: float32 [16, 512, 768], P('shard', 'expert')
- prior_logits_gradient: float32 [16, 512, 12], P('shard', 'expert')
- query_grad: float32 [768, 768], P('shard')
- key_grad: float32 [768, 768], P('shard')
- value_grad: float32 [768, 768], P('shard')
- output_grad: float32 [768, 768], P('shard')
- router_grad: float32 [768, 12], P('shard')
- const_grad: float32 [768, 2], P('shard')
- attn_gain_grad: float32 [768], P('shard')
- moe_gain_grad: float32 [768], P('shard')
- gate_grad: float32 [8, 768, 2048], P('expert', 'shard')
- up_grad: float32 [8, 768, 2048], P('expert', 'shard')
- down_grad: float32 [8, 2048, 768], P('expert', 'shard')
Inputs may be any that keep to these rules, and one draw needn't show every extreme that they name: `routes`: each token names two different experts. In each aligned block of 256 positions of a sequence no expert is named more than 64 times, and some expert below 8 exactly 64 times. `segment_ids`: ids never fall along a sequence; each document has at most 256 positions, and one has exactly 256.
All inputs are finite; a program needn't handle non-finite values.
Results may differ from a plain program's by a relative error of at most 0.035.
Values may be sent and summed in bfloat16 or wider, within the bound.
No kernel may reach another device: no remote copies, remote signals or barrier semaphores. Data moves between devices by JAX's collectives and lax.ppermute only.
A program may use at most 128 MiB of HBM per device.

v0:
```python
import math

import jax
import jax.numpy as jnp
from jax import lax
from jax.sharding import PartitionSpec as P

HEADS = 12
EXPERTS = 8
CAP = 64


norm_eps = 1e-06
masked_fill = -1e30


def rotary(values, positions, direction):
    dims_in = values.shape
    heads_view = values.reshape(dims_in[:-1] + (HEADS, dims_in[-1] // HEADS))
    half_size = heads_view.shape[-1] // 2
    frequency = jnp.exp(
        jnp.arange(half_size, dtype=jnp.float32) * (-2.0 * math.log(10000.0) / (2 * half_size))
    )
    angles = positions.astype(jnp.float32)[:, None] * frequency[None, :]
    cosine = jnp.cos(angles)[:, None, :]
    sine_part = direction * jnp.sin(angles)[:, None, :]
    first_half = heads_view[..., :half_size]
    second_half = heads_view[..., half_size:]
    turned = jnp.concatenate(
        [
            first_half * cosine - second_half * sine_part,
            second_half * cosine + first_half * sine_part,
        ],
        axis=-1,
    )
    return turned.reshape(dims_in)


def rms_parts(values):
    inverse = lax.rsqrt(jnp.mean(values * values, axis=-1, keepdims=True) + norm_eps)
    return (values * inverse, inverse)


def rms_back(grad_scaled, values, inverse):
    inner_mean = jnp.mean(grad_scaled * values, axis=-1, keepdims=True)
    return inverse * grad_scaled - values * inverse * inverse * inverse * inner_mean


def block_scores(query_heads, keys_all, segment_row, query_pos, query_seg, key_start, width_block):
    key_block = lax.dynamic_slice_in_dim(keys_all, key_start, width_block, 0)
    key_heads = key_block.reshape(width_block, HEADS, key_block.shape[-1] // HEADS)
    raw_scores = jnp.einsum(
        "qhd,khd->hqk", query_heads, key_heads, preferred_element_type=jnp.float32
    )
    scaled = raw_scores * key_heads.shape[-1] ** (-0.5)
    key_pos = key_start + jnp.arange(width_block, dtype=jnp.int32)
    key_seg = lax.dynamic_slice_in_dim(segment_row, key_start, width_block, 0)
    allowed = (key_pos[None, :] <= query_pos[:, None]) & (key_seg[None, :] == query_seg[:, None])
    return (scaled, allowed[None], key_heads)


def attend_forward(query_rot, keys_all, values_all, segment_row, offset, block_count, width_block):
    row_count = query_rot.shape[0]
    query_heads = query_rot.reshape(row_count, HEADS, -1)
    query_pos = offset + jnp.arange(row_count, dtype=jnp.int32)
    query_seg = lax.dynamic_slice_in_dim(segment_row, offset, row_count, 0)

    def gather_stats(number, state_pair):
        running_max, running_sum = state_pair
        scaled, allowed, key_heads = block_scores(
            query_heads,
            keys_all,
            segment_row,
            query_pos,
            query_seg,
            number * width_block,
            width_block,
        )
        masked = jnp.where(allowed, scaled, masked_fill)
        new_max = jnp.maximum(running_max, jnp.max(masked, axis=-1))
        exp_terms = jnp.where(allowed, jnp.exp(masked - new_max[..., None]), 0.0)
        return (new_max, running_sum * jnp.exp(running_max - new_max) + jnp.sum(exp_terms, axis=-1))

    start_max = jnp.full((HEADS, row_count), masked_fill, jnp.float32)
    start_sum = jnp.zeros((HEADS, row_count), jnp.float32)
    final_max, final_sum = lax.fori_loop(0, block_count, gather_stats, (start_max, start_sum))
    log_total = final_max + jnp.log(final_sum)

    def gather_output(number, running_out):
        key_start = number * width_block
        scaled, allowed, key_heads = block_scores(
            query_heads, keys_all, segment_row, query_pos, query_seg, key_start, width_block
        )
        weights = jnp.where(allowed, jnp.exp(scaled - log_total[..., None]), 0.0).astype(
            jnp.bfloat16
        )
        value_heads = lax.dynamic_slice_in_dim(values_all, key_start, width_block, 0).reshape(
            width_block, HEADS, -1
        )
        return running_out + jnp.einsum(
            "hqk,khd->qhd", weights, value_heads, preferred_element_type=jnp.float32
        )

    start_out = jnp.zeros((row_count, HEADS, query_heads.shape[-1]), jnp.float32)
    attention_output = lax.fori_loop(0, block_count, gather_output, start_out)
    return (attention_output.reshape(row_count, -1), log_total)


def attend_backward(
    query_rot,
    keys_all,
    values_all,
    segment_row,
    log_total,
    delta_sum,
    grad_low,
    offset,
    block_count,
    width_block,
):
    row_count = query_rot.shape[0]
    key_total = keys_all.shape[0]
    model_width = keys_all.shape[1]
    query_heads = query_rot.reshape(row_count, HEADS, -1)
    grad_heads = grad_low.reshape(row_count, HEADS, -1)
    query_pos = offset + jnp.arange(row_count, dtype=jnp.int32)
    query_seg = lax.dynamic_slice_in_dim(segment_row, offset, row_count, 0)
    score_scale = query_heads.shape[-1] ** (-0.5)

    def block_parts(number):
        key_start = number * width_block
        scaled, allowed, key_heads = block_scores(
            query_heads, keys_all, segment_row, query_pos, query_seg, key_start, width_block
        )
        prob_block = jnp.where(allowed, jnp.exp(scaled - log_total[..., None]), 0.0)
        value_heads = lax.dynamic_slice_in_dim(values_all, key_start, width_block, 0).reshape(
            width_block, HEADS, -1
        )
        grad_probs = jnp.einsum(
            "qhd,khd->hqk", grad_heads, value_heads, preferred_element_type=jnp.float32
        )
        grad_raw = (prob_block * (grad_probs - delta_sum[..., None]) * score_scale).astype(
            jnp.bfloat16
        )
        return (key_start, key_heads, prob_block, grad_raw)

    start_query = jnp.zeros((row_count, HEADS, query_heads.shape[-1]), jnp.float32)

    def accumulate(number, state_all):
        grad_query, grad_keys, grad_values = state_all
        key_start, key_heads, prob_block, grad_raw = block_parts(number)
        grad_query = grad_query + jnp.einsum(
            "hqk,khd->qhd", grad_raw, key_heads, preferred_element_type=jnp.float32
        )
        key_part = jnp.einsum(
            "hqk,qhd->khd", grad_raw, query_heads, preferred_element_type=jnp.float32
        )
        value_part = jnp.einsum(
            "hqk,qhd->khd",
            prob_block.astype(jnp.bfloat16),
            grad_heads,
            preferred_element_type=jnp.float32,
        )
        grad_keys = lax.dynamic_update_slice_in_dim(
            grad_keys, key_part.reshape(width_block, -1), key_start, 0
        )
        grad_values = lax.dynamic_update_slice_in_dim(
            grad_values, value_part.reshape(width_block, -1), key_start, 0
        )
        return (grad_query, grad_keys, grad_values)

    start_state = (
        start_query,
        jnp.zeros((key_total, model_width), jnp.float32),
        jnp.zeros((key_total, model_width), jnp.float32),
    )
    grad_query, grad_keys, grad_values = lax.fori_loop(0, block_count, accumulate, start_state)
    return (grad_query.reshape(row_count, -1), grad_keys, grad_values)


def body(
    tokens,
    segment_ids,
    routes,
    earlier_logits,
    out_cotangent,
    query_weight,
    key_weight,
    value_weight,
    output_weight,
    router_weight,
    const_vectors,
    attn_gain,
    moe_gain,
    gate_weight,
    up_weight,
    down_weight,
):
    (
        query_weight_wide,
        key_weight_wide,
        value_weight_wide,
        output_weight_wide,
        router_weight_wide,
        const_full,
        gain_attn,
        gain_moe,
    ) = (
        lax.all_gather(query_weight, "shard", axis=0, tiled=True),
        lax.all_gather(key_weight, "shard", axis=0, tiled=True),
        lax.all_gather(value_weight, "shard", axis=0, tiled=True),
        lax.all_gather(output_weight, "shard", axis=0, tiled=True),
        lax.all_gather(router_weight, "shard", axis=0, tiled=True),
        lax.all_gather(const_vectors, "shard", axis=0, tiled=True),
        lax.all_gather(attn_gain, "shard", axis=0, tiled=True),
        lax.all_gather(moe_gain, "shard", axis=0, tiled=True),
    )
    gate_full, up_full, down_full = (
        lax.all_gather(gate_weight, "shard", axis=1, tiled=True),
        lax.all_gather(up_weight, "shard", axis=1, tiled=True),
        lax.all_gather(down_weight, "shard", axis=1, tiled=True),
    )
    seq_count, pos_count, model_width = tokens.shape
    expert_pos = lax.axis_index("expert")
    offset = expert_pos * pos_count
    width_block = math.gcd(pos_count, 128)
    block_count = (expert_pos + 1) * (pos_count // width_block)
    positions = offset + jnp.arange(pos_count, dtype=jnp.int32)
    tokens_wide = tokens.astype(jnp.float32)
    scaled_one, inverse_one = rms_parts(tokens_wide)
    attn_gain_wide = gain_attn.astype(jnp.float32)
    normalized_first = (scaled_one * attn_gain_wide).astype(jnp.bfloat16)
    query_unrotated = jnp.einsum(
        "ibg,gv->ibv", normalized_first, query_weight_wide, preferred_element_type=jnp.float32
    )
    key_unrotated = jnp.einsum(
        "ibg,gv->ibv", normalized_first, key_weight_wide, preferred_element_type=jnp.float32
    )
    value_projected = jnp.einsum(
        "ibg,gv->ibv", normalized_first, value_weight_wide, preferred_element_type=jnp.float32
    )
    query_rot = rotary(query_unrotated, positions, 1.0).astype(jnp.bfloat16)
    key_rot = rotary(key_unrotated, positions, 1.0).astype(jnp.bfloat16)
    value_low = value_projected.astype(jnp.bfloat16)
    keys_all, values_all = (
        lax.all_gather(key_rot, "expert", axis=1, tiled=True),
        lax.all_gather(value_low, "expert", axis=1, tiled=True),
    )

    def forward_one(packed):
        return attend_forward(
            packed[0], packed[1], packed[2], packed[3], offset, block_count, width_block
        )

    attention_output, log_total = lax.map(
        forward_one, (query_rot, keys_all, values_all, segment_ids)
    )
    attention_output_narrow = attention_output.astype(jnp.bfloat16)
    projected_rows = jnp.einsum(
        "ibg,gv->ibv",
        attention_output_narrow,
        output_weight_wide,
        preferred_element_type=jnp.float32,
    )
    middle = tokens_wide + projected_rows
    scaled_two, inverse_two = rms_parts(middle)
    moe_gain_wide = gain_moe.astype(jnp.float32)
    normed_two = scaled_two * moe_gain_wide
    normalized_narrow = normed_two.astype(jnp.bfloat16)
    router_logits = (
        jnp.einsum(
            "ibg,gv->ibv", normalized_narrow, router_weight_wide, preferred_element_type=jnp.float32
        )
        + earlier_logits
    )
    chosen = jnp.take_along_axis(router_logits, routes, axis=-1)
    gate_probs = jax.nn.softmax(chosen, axis=-1)
    slot_count = seq_count * CAP
    route_entries = routes.reshape(seq_count, pos_count * 2)
    one_hot = (route_entries[..., None] == jnp.arange(EXPERTS, dtype=jnp.int32)).astype(jnp.int32)
    entry_ranks = jnp.cumsum(one_hot, axis=1) - one_hot
    slot_rank = jnp.sum(entry_ranks * one_hot, axis=-1)
    is_real = route_entries < EXPERTS
    destination = jnp.where(
        is_real,
        route_entries * slot_count
        + jnp.arange(seq_count, dtype=jnp.int32)[:, None] * CAP
        + slot_rank,
        EXPERTS * slot_count,
    ).reshape(-1)
    entry_rows = jnp.repeat(normalized_narrow.reshape(-1, model_width), 2, axis=0)
    send_rows = (
        jnp.zeros((EXPERTS * slot_count + 1, model_width), jnp.bfloat16)
        .at[destination]
        .set(entry_rows)[:-1]
        .reshape(EXPERTS, 1, slot_count, model_width)
    )
    received = lax.all_to_all(send_rows, "expert", split_axis=0, concat_axis=1, tiled=True)
    gate_pre = jnp.einsum("ensi,eif->ensf", received, gate_full, preferred_element_type=jnp.float32)
    up_pre = jnp.einsum("ensi,eif->ensf", received, up_full, preferred_element_type=jnp.float32)
    hidden = (jax.nn.silu(gate_pre) * up_pre).astype(jnp.bfloat16)
    result = jnp.einsum(
        "ensf,efi->ensi", hidden, down_full, preferred_element_type=jnp.float32
    ).astype(jnp.bfloat16)
    returned = lax.all_to_all(result, "expert", split_axis=1, concat_axis=0, tiled=True)
    zero_row = jnp.zeros((1, model_width), jnp.bfloat16)
    expert_vals = jnp.concatenate([returned.reshape(-1, model_width), zero_row], axis=0)[
        destination
    ].astype(jnp.float32)
    flat_routes = routes.reshape(-1)
    copy_rows = jnp.repeat(normed_two.reshape(-1, model_width), 2, axis=0)
    const_wide = const_full.astype(jnp.float32)
    is_copy = (flat_routes == EXPERTS + 1)[:, None]
    first_const = (flat_routes == EXPERTS + 2).astype(jnp.float32)[:, None]
    second_const = (flat_routes == EXPERTS + 3).astype(jnp.float32)[:, None]
    entry_vals = (
        expert_vals
        + jnp.where(is_copy, copy_rows, 0.0)
        + first_const * const_wide[:, 0][None, :]
        + second_const * const_wide[:, 1][None, :]
    )
    entry_vals = entry_vals.reshape(seq_count, pos_count, 2, model_width)
    layer_out = middle + jnp.sum(gate_probs[..., None] * entry_vals, axis=2)
    grad_mixed = out_cotangent.astype(jnp.float32)
    grad_gates = jnp.sum(grad_mixed[:, :, None, :] * entry_vals, axis=-1)
    grad_chosen = gate_probs * (
        grad_gates - jnp.sum(gate_probs * grad_gates, axis=-1, keepdims=True)
    )
    choice_ids = jnp.arange(EXPERTS + 4, dtype=jnp.int32)
    prior_logits_gradient = jnp.sum(
        (routes[..., None] == choice_ids).astype(jnp.float32) * grad_chosen[..., None], axis=2
    )
    grad_entries = (gate_probs[..., None] * grad_mixed[:, :, None, :]).reshape(-1, model_width)
    send_grads = (
        jnp.zeros((EXPERTS * slot_count + 1, model_width), jnp.bfloat16)
        .at[destination]
        .set(grad_entries.astype(jnp.bfloat16))[:-1]
        .reshape(EXPERTS, 1, slot_count, model_width)
    )
    owner_grads = lax.all_to_all(send_grads, "expert", split_axis=0, concat_axis=1, tiled=True)
    sigmoid_gate = jax.nn.sigmoid(gate_pre)
    silu_gate = gate_pre * sigmoid_gate
    hidden_back = (silu_gate * up_pre).astype(jnp.bfloat16)
    grad_hidden = jnp.einsum(
        "ensd,efd->ensf", owner_grads, down_full, preferred_element_type=jnp.float32
    )
    grad_gate_pre = (
        grad_hidden * up_pre * sigmoid_gate * (1.0 + gate_pre * (1.0 - sigmoid_gate))
    ).astype(jnp.bfloat16)
    grad_up_pre = (grad_hidden * silu_gate).astype(jnp.bfloat16)
    down_part = jnp.einsum(
        "ensf,ensd->efd", hidden_back, owner_grads, preferred_element_type=jnp.float32
    )
    gate_part = jnp.einsum(
        "ensi,ensf->eif", received, grad_gate_pre, preferred_element_type=jnp.float32
    )
    up_part = jnp.einsum(
        "ensi,ensf->eif", received, grad_up_pre, preferred_element_type=jnp.float32
    )
    grad_rows = (
        jnp.einsum("ensf,eif->ensi", grad_gate_pre, gate_full, preferred_element_type=jnp.float32)
        + jnp.einsum("ensf,eif->ensi", grad_up_pre, up_full, preferred_element_type=jnp.float32)
    ).astype(jnp.bfloat16)
    rows_back = lax.all_to_all(grad_rows, "expert", split_axis=1, concat_axis=0, tiled=True)
    gate_grad, up_grad, down_grad = (
        lax.psum_scatter(
            gate_part.astype(jnp.bfloat16), "shard", scatter_dimension=1, tiled=True
        ).astype(jnp.float32),
        lax.psum_scatter(
            up_part.astype(jnp.bfloat16), "shard", scatter_dimension=1, tiled=True
        ).astype(jnp.float32),
        lax.psum_scatter(
            down_part.astype(jnp.bfloat16), "shard", scatter_dimension=1, tiled=True
        ).astype(jnp.float32),
    )
    grad_row_entries = jnp.concatenate([rows_back.reshape(-1, model_width), zero_row], axis=0)[
        destination
    ].astype(jnp.float32)
    grad_copy = jnp.where(is_copy, grad_entries, 0.0)
    router_widened = router_weight_wide.astype(jnp.float32)
    grad_normed_two = jnp.sum(
        (grad_row_entries + grad_copy).reshape(seq_count, pos_count, 2, model_width), axis=2
    ) + jnp.einsum(
        "hwk,ok->hwo", prior_logits_gradient, router_widened, precision=lax.Precision.HIGHEST
    )
    router_part = jnp.einsum(
        "vrx,vrb->xb",
        normalized_narrow.astype(jnp.float32),
        prior_logits_gradient,
        precision=lax.Precision.HIGHEST,
    )
    const_part = jnp.stack(
        [jnp.sum(first_const * grad_entries, axis=0), jnp.sum(second_const * grad_entries, axis=0)],
        axis=-1,
    )
    moe_gain_part = jnp.sum(grad_normed_two * scaled_two, axis=(0, 1))
    grad_middle = grad_mixed + rms_back(grad_normed_two * moe_gain_wide, middle, inverse_two)
    gradient_projected = grad_middle.astype(jnp.bfloat16)
    output_part = jnp.einsum(
        "vrx,vrb->xb",
        attention_output_narrow,
        gradient_projected,
        preferred_element_type=jnp.float32,
    )
    grad_attended = jnp.einsum(
        "hwk,ok->hwo", gradient_projected, output_weight_wide, preferred_element_type=jnp.float32
    ).astype(jnp.bfloat16)
    delta_rows = jnp.sum(
        (grad_attended.astype(jnp.float32) * attention_output).reshape(
            seq_count, pos_count, HEADS, -1
        ),
        axis=-1,
    )
    delta_sum = jnp.transpose(delta_rows, (0, 2, 1))

    def backward_one(packed):
        return attend_backward(
            packed[0],
            packed[1],
            packed[2],
            packed[3],
            packed[4],
            packed[5],
            packed[6],
            offset,
            block_count,
            width_block,
        )

    grad_query_rot, grad_keys_all, grad_values_all = lax.map(
        backward_one,
        (query_rot, keys_all, values_all, segment_ids, log_total, delta_sum, grad_attended),
    )
    grad_keys, grad_values = (
        lax.psum_scatter(
            grad_keys_all.astype(jnp.bfloat16), "expert", scatter_dimension=1, tiled=True
        ).astype(jnp.float32),
        lax.psum_scatter(
            grad_values_all.astype(jnp.bfloat16), "expert", scatter_dimension=1, tiled=True
        ).astype(jnp.float32),
    )
    gradient_query_unrotated = rotary(grad_query_rot, positions, -1.0).astype(jnp.bfloat16)
    gradient_key_unrotated = rotary(grad_keys, positions, -1.0).astype(jnp.bfloat16)
    gradient_value_narrow = grad_values.astype(jnp.bfloat16)
    query_part = jnp.einsum(
        "vrx,vrb->xb",
        normalized_first,
        gradient_query_unrotated,
        preferred_element_type=jnp.float32,
    )
    key_part = jnp.einsum(
        "vrx,vrb->xb", normalized_first, gradient_key_unrotated, preferred_element_type=jnp.float32
    )
    value_part = jnp.einsum(
        "vrx,vrb->xb", normalized_first, gradient_value_narrow, preferred_element_type=jnp.float32
    )
    grad_normed_one = jnp.einsum(
        "hwk,ok->hwo",
        gradient_query_unrotated,
        query_weight_wide,
        preferred_element_type=jnp.float32,
    )
    grad_normed_one = grad_normed_one + jnp.einsum(
        "hwk,ok->hwo", gradient_key_unrotated, key_weight_wide, preferred_element_type=jnp.float32
    )
    grad_normed_one = grad_normed_one + jnp.einsum(
        "hwk,ok->hwo", gradient_value_narrow, value_weight_wide, preferred_element_type=jnp.float32
    )
    attn_gain_part = jnp.sum(grad_normed_one * scaled_one, axis=(0, 1))
    tokens_grad = grad_middle + rms_back(grad_normed_one * attn_gain_wide, tokens_wide, inverse_one)
    layer_parts = (
        lax.psum_scatter(
            query_part.astype(jnp.bfloat16), "shard", scatter_dimension=0, tiled=True
        ).astype(jnp.float32),
        lax.psum_scatter(
            key_part.astype(jnp.bfloat16), "shard", scatter_dimension=0, tiled=True
        ).astype(jnp.float32),
        lax.psum_scatter(
            value_part.astype(jnp.bfloat16), "shard", scatter_dimension=0, tiled=True
        ).astype(jnp.float32),
        lax.psum_scatter(
            output_part.astype(jnp.bfloat16), "shard", scatter_dimension=0, tiled=True
        ).astype(jnp.float32),
        lax.psum_scatter(
            router_part.astype(jnp.bfloat16), "shard", scatter_dimension=0, tiled=True
        ).astype(jnp.float32),
        lax.psum_scatter(
            const_part.astype(jnp.bfloat16), "shard", scatter_dimension=0, tiled=True
        ).astype(jnp.float32),
        lax.psum_scatter(
            attn_gain_part.astype(jnp.bfloat16), "shard", scatter_dimension=0, tiled=True
        ).astype(jnp.float32),
        lax.psum_scatter(
            moe_gain_part.astype(jnp.bfloat16), "shard", scatter_dimension=0, tiled=True
        ).astype(jnp.float32),
    )
    layer_grads = (
        lax.psum(layer_parts[0].astype(jnp.bfloat16), "expert").astype(jnp.float32),
        lax.psum(layer_parts[1].astype(jnp.bfloat16), "expert").astype(jnp.float32),
        lax.psum(layer_parts[2].astype(jnp.bfloat16), "expert").astype(jnp.float32),
        lax.psum(layer_parts[3].astype(jnp.bfloat16), "expert").astype(jnp.float32),
        lax.psum(layer_parts[4].astype(jnp.bfloat16), "expert").astype(jnp.float32),
        lax.psum(layer_parts[5].astype(jnp.bfloat16), "expert").astype(jnp.float32),
        lax.psum(layer_parts[6].astype(jnp.bfloat16), "expert").astype(jnp.float32),
        lax.psum(layer_parts[7].astype(jnp.bfloat16), "expert").astype(jnp.float32),
    )
    return (
        layer_out.astype(jnp.bfloat16),
        tokens_grad,
        prior_logits_gradient,
        layer_grads[0],
        layer_grads[1],
        layer_grads[2],
        layer_grads[3],
        layer_grads[4],
        layer_grads[5],
        layer_grads[6],
        layer_grads[7],
        gate_grad,
        up_grad,
        down_grad,
    )


def solution(mesh):
    in_specs = (
        P("shard", "expert", None),
        P("shard", None),
        P("shard", "expert", None),
        P("shard", "expert", None),
        P("shard", "expert", None),
        P("shard", None),
        P("shard", None),
        P("shard", None),
        P("shard", None),
        P("shard", None),
        P("shard", None),
        P("shard"),
        P("shard"),
        P("expert", "shard", None),
        P("expert", "shard", None),
        P("expert", "shard", None),
    )
    out_specs = (
        P("shard", "expert", None),
        P("shard", "expert", None),
        P("shard", "expert", None),
        P("shard", None),
        P("shard", None),
        P("shard", None),
        P("shard", None),
        P("shard", None),
        P("shard", None),
        P("shard"),
        P("shard"),
        P("expert", "shard", None),
        P("expert", "shard", None),
        P("expert", "shard", None),
    )
    return jax.shard_map(body, mesh=mesh, in_specs=in_specs, out_specs=out_specs, check_vma=False)
```

profile of v0, /device:TPU:0, one launch (start us, length us, event | category | flops | bytes accessed | tf_op | source)
XLA Modules:
  0.0 1439.1 jit_solution(7292282806118360613)
XLA Ops:
  13.7 35.1 %all-reduce.7 = (bf16[768]{0:T(1024)(128)(2,1)S(1)}, bf16[768]{0:T(1024)(128)(2,1)S(1)}) all-reduce(bf16[768]{0:T(1024)(128)(2,1)S(1)} %dynamic-update-slice, bf16[768]{0:T(1024)(128)(2,1)S(1)} %dynamic-update-slice.1), channel_id=1, replica_groups=mesh['expert'=2,'shard'=16] {'shard'}, use_global_device_ids=true, to_apply=%add.2 | all-reduce | flops 1536 | bytes 6144
  54.7 17.4 %all-gather.1 = bf16[16,48,12]{1,2,0:T(8,128)(2,1)S(1)} all-gather(bf16[1,48,12]{1,2,0:T(8,128)(2,1)S(1)} %bitcast.384), channel_id=1, replica_groups=mesh['expert'=2,'shard'=16] {'shard'}, dimensions={0}, use_global_device_ids=true | all-gather | bytes 19584 | tf_op jit(solution)/shard_map/all_gather | solution.py:213
  73.1 19.0 %all-gather.2 = bf16[16,48,2]{1,2,0:T(2,128)(2,1)S(1)} all-gather(bf16[1,48,2]{1,2,0:T(2,128)(2,1)S(1)} %bitcast.385), channel_id=1, replica_groups=mesh['expert'=2,'shard'=16] {'shard'}, dimensions={0}, use_global_device_ids=true | all-gather | bytes 3264 | tf_op jit(solution)/shard_map/all_gather | solution.py:214
  97.4 12.0 all-gather
  112.2 18.1 %all-gather.13.cloned.1.call-done = bf16[768,768]{1,0:T(8,128)(2,1)} async-done(((bf16[48,768]{1,0:T(8,128)(2,1)}), bf16[768,768]{1,0:T(8,128)(2,1)}) %all-gather.13.cloned.1.call-update) | async-done | bytes 1179664 | tf_op jit(solution)/shard_map/all_gather | solution.py:210
  134.3 12.1 all_gather.43
  206.5 64.6 %all-gather.19.cloned.1.call-done = bf16[4,768,2048]{2,1,0:T(8,128)(2,1)} async-done(((bf16[4,48,2048]{2,1,0:T(8,128)(2,1)}), bf16[4,768,2048]{2,1,0:T(8,128)(2,1)}) %all-gather.19.cloned.1.call-update) | async-done | bytes 12582928 | tf_op jit(solution)/shard_map/all_gather | solution.py:219
  279.7 92.2 %all-gather.23.cloned.1.call-done = bf16[4,2048,768]{2,1,0:T(8,128)(2,1)} async-done(((bf16[4,128,768]{2,1,0:T(8,128)(2,1)}), bf16[4,2048,768]{2,1,0:T(8,128)(2,1)}) %all-gather.23.cloned.1.call-update) | async-done | bytes 12582928 | tf_op jit(solution)/shard_map/all_gather | solution.py:221
  382.8 90.1 %all-gather.21.cloned.1.call-done = bf16[4,768,2048]{2,1,0:T(8,128)(2,1)} async-done(((bf16[4,48,2048]{2,1,0:T(8,128)(2,1)}), bf16[4,768,2048]{2,1,0:T(8,128)(2,1)}) %all-gather.21.cloned.1.call-update) | async-done | bytes 12582928 | tf_op jit(solution)/shard_map/all_gather | solution.py:220
  472.9 13.3 multiply_convert_fusion.2
  551.0 12.2 add_reduce_fusion
  571.2 12.1 while.64
  586.2 25.6 %reduce-scatter.16.cloned.1.call-done = bf16[1,256,768]{1,2,0:T(8,128)(2,1)} async-done(((bf16[1,512,768]{1,2,0:T(8,128)(2,1)}), bf16[1,256,768]{1,2,0:T(8,128)(2,1)}) %reduce-scatter.16.cloned.1.call-update) | async-done | bytes 393232 | tf_op jit(solution)/shard_map/reduce_scatter | solution.py:435
  617.4 14.8 %reduce-scatter.18.cloned.1.call-done = bf16[1,256,768]{1,2,0:T(8,128)(2,1)} async-done(((bf16[1,512,768]{1,2,0:T(8,128)(2,1)}), bf16[1,256,768]{1,2,0:T(8,128)(2,1)}) %reduce-scatter.18.cloned.1.call-update) | async-done | bytes 393232 | tf_op jit(solution)/shard_map/reduce_scatter | solution.py:438
  638.1 55.8 %reduce-scatter.26.cloned.1.call-done = bf16[48,768]{1,0:T(8,128)(2,1)} async-done(((bf16[768,768]{1,0:T(8,128)(2,1)}), bf16[48,768]{1,0:T(8,128)(2,1)}) %reduce-scatter.26.cloned.1.call-update) | async-done | bytes 73744 | tf_op jit(solution)/shard_map/reduce_scatter | solution.py:481
  693.9 61.4 %reduce-scatter.20.cloned.1.call-done = bf16[48,768]{1,0:T(8,128)(2,1)} async-done(((bf16[768,768]{1,0:T(8,128)(2,1)}), bf16[48,768]{1,0:T(8,128)(2,1)}) %reduce-scatter.20.cloned.1.call-update) | async-done | bytes 73744 | tf_op jit(solution)/shard_map/reduce_scatter | solution.py:472
  755.3 61.2 %reduce-scatter.22.cloned.1.call-done = bf16[48,768]{1,0:T(8,128)(2,1)} async-done(((bf16[768,768]{1,0:T(8,128)(2,1)}), bf16[48,768]{1,0:T(8,128)(2,1)}) %reduce-scatter.22.cloned.1.call-update) | async-done | bytes 73744 | tf_op jit(solution)/shard_map/reduce_scatter | solution.py:475
  816.5 61.4 %reduce-scatter.24.cloned.1.call-done = bf16[48,768]{1,0:T(8,128)(2,1)} async-done(((bf16[768,768]{1,0:T(8,128)(2,1)}), bf16[48,768]{1,0:T(8,128)(2,1)}) %reduce-scatter.24.cloned.1.call-update) | async-done | bytes 73744 | tf_op jit(solution)/shard_map/reduce_scatter | solution.py:478
  905.3 28.4 %reduce-scatter.36.cloned.1.call-done = bf16[48,2]{1,0:T(8,128)(2,1)} async-done(((bf16[768,2]{1,0:T(8,128)(2,1)}), bf16[48,2]{1,0:T(8,128)(2,1)}) %reduce-scatter.36.cloned.1.call-update) | async-done | bytes 208
  934.5 55.0 %reduce-scatter.34.cloned.1.call-done = bf16[48,12]{1,0:T(8,128)(2,1)} async-done(((bf16[768,12]{1,0:T(8,128)(2,1)}), bf16[48,12]{1,0:T(8,128)(2,1)}) %reduce-scatter.34.cloned.1.call-update) | async-done | bytes 1168
  993.9 29.5 %all-reduce.6 = (bf16[768]{0:T(1024)(128)(2,1)S(1)}, bf16[768]{0:T(1024)(128)(2,1)S(1)}) all-reduce(bf16[768]{0:T(1024)(128)(2,1)S(1)} %get-tuple-element.529, bf16[768]{0:T(1024)(128)(2,1)S(1)} %copy-done.56), channel_id=11, replica_groups=mesh['expert'=2,'shard'=16] {'shard'}, use_global_device_ids=true, to_apply=%region_42.43.clone | all-reduce | flops 1536 | bytes 6144
  1038.3 115.3 %reduce-scatter.28.cloned.1.call-done = bf16[4,48,2048]{2,1,0:T(8,128)(2,1)} async-done(((bf16[4,768,2048]{2,1,0:T(8,128)(2,1)}), bf16[4,48,2048]{2,1,0:T(8,128)(2,1)}) %reduce-scatter.28.cloned.1.call-update) | async-done | bytes 786448 | tf_op jit(solution)/shard_map/reduce_scatter | solution.py:366
  1156.0 135.6 %reduce-scatter.30.cloned.1.call-done = bf16[4,48,2048]{2,1,0:T(8,128)(2,1)} async-done(((bf16[4,768,2048]{2,1,0:T(8,128)(2,1)}), bf16[4,48,2048]{2,1,0:T(8,128)(2,1)}) %reduce-scatter.30.cloned.1.call-update) | async-done | bytes 786448 | tf_op jit(solution)/shard_map/reduce_scatter | solution.py:369
  1294.1 135.8 %reduce-scatter.32.cloned.1.call-done = bf16[4,128,768]{2,1,0:T(8,128)(2,1)} async-done(((bf16[4,2048,768]{2,1,0:T(8,128)(2,1)}), bf16[4,128,768]{2,1,0:T(8,128)(2,1)}) %reduce-scatter.32.cloned.1.call-update) | async-done | bytes 786448 | tf_op jit(solution)/shard_map/reduce_scatter | solution.py:372
  (398 shorter events, 267.5 us)
Async XLA Ops:
  7.2 88.4 %all-gather.11.cloned.1.call-start = ((), (), s32[]{:S(2)}) async-start(), calls=%async_computation.15 | async-start | bytes 1253376 | tf_op jit(solution)/shard_map/all_gather | solution.py:211
  8.0 102.6 %all-gather.15.cloned.1.call-start = ((), (), s32[]{:S(2)}) async-start(), calls=%async_computation.17 | async-start | bytes 1253376 | tf_op jit(solution)/shard_map/all_gather | solution.py:209
  8.7 121.5 %all-gather.13.cloned.1.call-start = ((), (), s32[]{:S(2)}) async-start(), calls=%async_computation.16 | async-start | bytes 1253376 | tf_op jit(solution)/shard_map/all_gather | solution.py:210
  9.4 160.1 %all-gather.17.cloned.1.call-start = ((), (), s32[]{:S(2)}) async-start(), calls=%async_computation.18 | async-start | bytes 1253376 | tf_op jit(solution)/shard_map/all_gather | solution.py:212
  10.0 261.0 %all-gather.19.cloned.1.call-start = ((), (), s32[]{:S(2)}) async-start(), calls=%async_computation.19 | async-start | bytes 13369344 | tf_op jit(solution)/shard_map/all_gather | solution.py:219
  10.6 361.3 %all-gather.23.cloned.1.call-start = ((), (), s32[]{:S(2)}) async-start(), calls=%async_computation.21 | async-start | bytes 13369344 | tf_op jit(solution)/shard_map/all_gather | solution.py:221
  11.2 461.7 %all-gather.21.cloned.1.call-start = ((), (), s32[]{:S(2)}) async-start(), calls=%async_computation.20 | async-start | bytes 13369344 | tf_op jit(solution)/shard_map/all_gather | solution.py:220
  158.5 364.0 %copy-start.2 = (f32[256,12,64]{0,2,1:T(8,128)}, f32[256,12,64]{0,2,1:T(8,128)S(1)}, u32[]{:S(2)}) copy-start(f32[256,12,64]{0,2,1:T(8,128)S(1)} %get-tuple-element.259) | copy-start | bytes 2359300
  184.6 17.3 %all-to-all-start = ((bf16[8,1,64,768]{3,2,1,0:T(8,128)(2,1)}), bf16[8,1,64,768]{3,2,1,0:T(8,128)(2,1)}, u32[]{:S(2)}, u32[]{:S(2)}) async-start(bf16[8,1,64,768]{3,2,1,0:T(8,128)(2,1)} %bitcast.365), calls=%async_computation | async-start | bytes 1572864 | tf_op jit(solution)/shard_map/all_to_all | solution.py:298
  201.9 77.8 %all-to-all-start.2 = ((bf16[8,1,64,768]{3,2,1,0:T(8,128)(2,1)}), bf16[8,1,64,768]{3,2,1,0:T(8,128)(2,1)}, u32[]{:S(2)}, u32[]{:S(2)}) async-start(bf16[8,1,64,768]{3,2,1,0:T(8,128)(2,1)} %bitcast.366), calls=%async_computation.2 | async-start | bytes 1572864 | tf_op jit(solution)/shard_map/all_to_all | solution.py:340
  489.1 24.3 %all-to-all-start.1 = ((bf16[4,2,64,768]{3,2,0,1:T(8,128)(2,1)}), bf16[4,2,64,768]{3,2,0,1:T(8,128)(2,1)}, u32[]{:S(2)}, u32[]{:S(2)}) async-start(bf16[4,2,64,768]{3,2,0,1:T(8,128)(2,1)} %copy.208), calls=%async_computation.1 | async-start | bytes 1572864 | tf_op jit(solution)/shard_map/all_to_all | solution.py:305
  513.4 19.6 %all-to-all-start.3 = ((bf16[4,2,64,768]{3,2,0,1:T(8,128)(2,1)}), bf16[4,2,64,768]{3,2,0,1:T(8,128)(2,1)}, u32[]{:S(2)}, u32[]{:S(2)}) async-start(bf16[4,2,64,768]{3,2,0,1:T(8,128)(2,1)} %copy.215), calls=%async_computation.3 | async-start | bytes 1572864 | tf_op jit(solution)/shard_map/all_to_all | solution.py:364
  517.7 94.1 %reduce-scatter.16.cloned.1.call-start = ((), (), s32[]{:S(2)}) async-start(), calls=%async_computation.22 | async-start | bytes 1179648 | tf_op jit(solution)/shard_map/reduce_scatter | solution.py:435
  583.3 48.9 %reduce-scatter.18.cloned.1.call-start = ((), (), s32[]{:S(2)}) async-start(), calls=%async_computation.23 | async-start | bytes 1179648 | tf_op jit(solution)/shard_map/reduce_scatter | solution.py:438
  584.0 109.8 %reduce-scatter.26.cloned.1.call-start = ((), (), s32[]{:S(2)}) async-start(), calls=%async_computation.27 | async-start | bytes 1253376 | tf_op jit(solution)/shard_map/reduce_scatter | solution.py:481
  586.0 169.3 %reduce-scatter.20.cloned.1.call-start = ((), (), s32[]{:S(2)}) async-start(), calls=%async_computation.24 | async-start | bytes 1253376 | tf_op jit(solution)/shard_map/reduce_scatter | solution.py:472
  615.6 200.9 %reduce-scatter.22.cloned.1.call-start = ((), (), s32[]{:S(2)}) async-start(), calls=%async_computation.25 | async-start | bytes 1253376 | tf_op jit(solution)/shard_map/reduce_scatter | solution.py:475
  617.4 260.5 %reduce-scatter.24.cloned.1.call-start = ((), (), s32[]{:S(2)}) async-start(), calls=%async_computation.26 | async-start | bytes 1253376 | tf_op jit(solution)/shard_map/reduce_scatter | solution.py:478
  634.9 298.8 %reduce-scatter.36.cloned.1.call-start = ((), (), s32[]{:S(2)}) async-start(), calls=%async_computation.32 | async-start | bytes 208896
  635.8 353.6 %reduce-scatter.34.cloned.1.call-start = ((), (), s32[]{:S(2)}) async-start(), calls=%async_computation.31 | async-start | bytes 208896
  638.0 393.9 %all-reduce.12.cloned.1.call-start = ((), (), s32[]{:S(2)}) async-start(), calls=%async_computation.33 | async-start | bytes 589824 | tf_op jit(solution)/shard_map/psum | solution.py:498
  877.9 275.6 %reduce-scatter.28.cloned.1.call-start = ((), (), s32[]{:S(2)}) async-start(), calls=%async_computation.28 | async-start | bytes 13369344 | tf_op jit(solution)/shard_map/reduce_scatter | solution.py:366
  885.5 406.1 %reduce-scatter.30.cloned.1.call-start = ((), (), s32[]{:S(2)}) async-start(), calls=%async_computation.29 | async-start | bytes 13369344 | tf_op jit(solution)/shard_map/reduce_scatter | solution.py:369
  894.8 535.1 %reduce-scatter.32.cloned.1.call-start = ((), (), s32[]{:S(2)}) async-start(), calls=%async_computation.30 | async-start | bytes 13369344 | tf_op jit(solution)/shard_map/reduce_scatter | solution.py:372
  (69 other events, 2023.2 us)
Sparse Core Ops, SparseCore 0:
  10.3 41.1 all-gather.10
  53.8 37.0 all-gather.14
  93.2 37.0 all-gather.12
  132.4 37.1 all-gather.16
  171.7 99.3 all-gather.18
  273.2 98.6 all-gather.22
  374.2 98.6 all-gather.20
  583.4 28.3 reduce-scatter.15
  614.6 17.5 reduce-scatter.17
  635.7 58.1 reduce-scatter.25
  698.1 57.1 reduce-scatter.19
  759.3 57.1 reduce-scatter.21
  820.7 57.1 reduce-scatter.23
  881.2 52.3 reduce-scatter.35
  937.0 52.3 reduce-scatter.33
  991.7 22.8 all-reduce.11
  1018.6 134.9 reduce-scatter.27
  1157.5 134.1 reduce-scatter.29
  1295.7 134.1 reduce-scatter.31
where the time goes:
time: 1450 us; the launch traced here: 1440 us
  waiting for transfers between devices  1030 us (71%)
  blocking collectives  130 us (9%)
  matrix products  106 us (7%)
  local copies, waits for them, and re-layouts  78.2 us (5%)
  other arithmetic  57.3 us (4%)
  starting transfers between devices  18.8 us (1%)
  between operations  16.8 us (1%)
    reduce_scatter x1, waiting for transfers between devices, body(): lax.psum_scatter(down_part.astype(jnp.bfloat16), 'shard', scatter_dimensi...  136 us
    reduce_scatter x1, waiting for transfers between devices, body(): lax.psum_scatter(up_part.astype(jnp.bfloat16), 'shard', scatter_dimension...  136 us
    reduce_scatter x1, waiting for transfers between devices, body(): lax.psum_scatter(gate_part.astype(jnp.bfloat16), 'shard', scatter_dimensi...  115 us
    all_gather x1, waiting for transfers between devices, body(): lax.all_gather(down_weight, 'shard', axis=1, tiled=True)  92.2 us
    all_gather x1, waiting for transfers between devices, body(): lax.all_gather(up_weight, 'shard', axis=1, tiled=True)  90.1 us
    unnamed x21, waiting for transfers between devices  88.6 us
    unnamed x2, blocking collectives  64.6 us
    all_gather x1, waiting for transfers between devices, body(): lax.all_gather(gate_weight, 'shard', axis=1, tiled=True)  64.6 us
  transfers between devices with their start and end apart: 23, of which 16 were waited for; matrix products, arithmetic and copies ran while one was open for 12% of the time, Pallas kernels for 0%

commit v1 on v0

--- a/solution.py
+++ b/solution.py
@@ -3,6 +3,8 @@
 import jax
 import jax.numpy as jnp
 from jax import lax
+from jax.experimental import pallas as pl
+from jax.experimental.pallas import tpu as pltpu
 from jax.sharding import PartitionSpec as P
 
 HEADS = 12
@@ -522,6 +524,613 @@
     )
 
 
+RING = 4
+PAIR = 2
+LOCAL = 4
+META = 16
+
+
+def z_pairs(step):
+    lines = PAIR * PAIR
+    return [
+        (z * lines + rest, (z + step) % RING * lines + rest)
+        for z in range(RING)
+        for rest in range(lines)
+    ]
+
+
+def along_z(values, step):
+    return lax.ppermute(values, "shard", z_pairs(step))
+
+
+def across_y(values):
+    return lax.ppermute(values, "shard", [(s, s ^ PAIR) for s in range(RING * PAIR * PAIR)])
+
+
+def across_core(values):
+    return lax.ppermute(values, "shard", [(s, s ^ 1) for s in range(RING * PAIR * PAIR)])
+
+
+def across_x(values):
+    return lax.ppermute(values, "expert", [(0, 1), (1, 0)])
+
+
+def gather_rows(own):
+    ring = [own]
+    for _ in range(RING - 1):
+        ring.append(along_z(ring[-1], 1))
+    return ring + [across_x(block) for block in ring]
+
+
+def reduce_rows(parts):
+    total = None
+    for step in reversed(range(RING)):
+        here = parts[step].astype(jnp.float32) + across_x(parts[RING + step]).astype(jnp.float32)
+        if total is not None:
+            here = here + along_z(total, -1).astype(jnp.float32)
+        total = here.astype(jnp.bfloat16)
+    return here
+
+
+def meta_rows(rows, width):
+    filled = jnp.concatenate(rows, axis=-1).reshape(len(rows) // 2, -1)
+    return jnp.pad(filled, ((0, META - filled.shape[0]), (0, width - filled.shape[1]))).astype(
+        jnp.bfloat16
+    )
+
+
+def dot_rows(left, right):
+    return lax.dot_general(left, right, (((1,), (0,)), ((), ())), preferred_element_type=jnp.float32)
+
+
+def dot_wide(left, right):
+    return lax.dot_general(left, right, (((1,), (1,)), ((), ())), preferred_element_type=jnp.float32)
+
+
+def dot_tall(left, right):
+    return lax.dot_general(left, right, (((0,), (0,)), ((), ())), preferred_element_type=jnp.float32)
+
+
+def owner_index(place, step, side, core):
+    return (
+        lax.rem(place[1] - step + RING, RING) * (PAIR * PAIR)
+        + (place[2] ^ side) * PAIR
+        + (place[3] ^ core)
+    )
+
+
+def prepare_kernel(place, *refs):
+    block_count = RING * PAIR
+    grads = refs[:block_count]
+    mixed = refs[block_count : block_count + 4]
+    downs = refs[block_count + 4 : block_count + 8]
+    pick_ref, slot_ref, back_ref, wide_ref, down_ref = refs[block_count + 8 :]
+    number = pl.program_id(0)
+    rows = pick_ref.shape[2]
+
+    @pl.when(number == 0)
+    def _():
+        later = lax.broadcasted_iota(jnp.int32, (rows, rows), 1)
+        earlier = lax.broadcasted_iota(jnp.int32, (rows, rows), 0)
+        before = jnp.where(earlier < later, 1.0, 0.0).astype(jnp.bfloat16)
+        wanted = (lax.broadcasted_iota(jnp.int32, (8, rows), 0) + place[0] * LOCAL).astype(
+            jnp.float32
+        )
+        inside = lax.broadcasted_iota(jnp.int32, (8, rows), 0) < LOCAL
+        ranks = lax.broadcasted_iota(jnp.int32, (CAP, rows), 0).astype(jnp.float32)
+        for block in range(block_count):
+            meta = grads[block][rows : rows + META, :].astype(jnp.float32)
+            first = meta[1:2, :rows]
+            second = meta[1:2, rows : 2 * rows]
+            named = jnp.where(((first == wanted) | (second == wanted)) & inside, 1.0, 0.0)
+            rank = dot_rows(named.astype(jnp.bfloat16), before)
+            pieces = []
+            for expert in range(LOCAL):
+                hit = (rank[expert : expert + 1] == ranks) & (named[expert : expert + 1] > 0.5)
+                pieces.append(jnp.where(hit, 1.0, 0.0))
+            pick = jnp.concatenate(pieces, axis=0).astype(jnp.bfloat16)
+            pick_ref[block] = pick
+            slot_ref[block] = dot_rows(pick, grads[block][:rows, :]).astype(jnp.bfloat16)
+
+    half = wide_ref.shape[2] // 2
+    for core in range(PAIR):
+        for side in range(PAIR):
+            piece = mixed[core * PAIR + side]
+            depth = piece.shape[3]
+            for step in range(RING):
+                start = pl.multiple_of(owner_index(place, step, side, core) * depth, 16)
+                wide_ref[0, pl.ds(start, depth), :half] = piece[step, 0, 0]
+                wide_ref[0, pl.ds(start, depth), half:] = piece[step, 1, 0]
+            own = downs[core * PAIR + side]
+            deep = own.shape[1]
+            local = (place[2] ^ side) * PAIR + (place[3] ^ core)
+            down_ref[0, pl.ds(pl.multiple_of(local * deep, 16), deep), :] = own[0]
+    width = slot_ref.shape[2]
+    mine = slot_ref[:, pl.ds(pl.multiple_of(number * CAP, CAP), CAP), :]
+    back_ref[0] = dot_wide(mine.reshape(block_count * CAP, width), down_ref[0])
+
+
+def expert_kernel(place, *refs):
+    block_count = RING * PAIR
+    tokens = refs[:block_count]
+    pick_ref, wide_ref, down_ref, back_ref = refs[block_count : block_count + 4]
+    rest = refs[block_count + 4 :]
+    slot_ref, hidden_ref, mixed_ref = rest[:3]
+    grad_refs = rest[3 : 3 + block_count]
+    out_refs = rest[3 + block_count : 3 + 2 * block_count]
+    out_slots, grad_slots, gate_grads = rest[3 + 2 * block_count :]
+    number = pl.program_id(0)
+    rows = pick_ref.shape[2]
+    width = slot_ref.shape[2]
+    half = wide_ref.shape[2] // 2
+
+    @pl.when(number == 0)
+    def _():
+        gate_grads[...] = jnp.zeros_like(gate_grads)
+        for block in range(block_count):
+            slot_ref[block] = dot_rows(pick_ref[block], tokens[block][:rows, :]).astype(
+                jnp.bfloat16
+            )
+
+    span = pl.ds(pl.multiple_of(number * CAP, CAP), CAP)
+    mine = slot_ref[:, span, :].reshape(block_count * CAP, width)
+    both = dot_rows(mine, wide_ref[0])
+    gate = both[:, :half]
+    up = both[:, half:]
+    sigmoid = 1.0 / (1.0 + jnp.exp(-gate))
+    silu = gate * sigmoid
+    hidden = silu * up
+    back = back_ref[0]
+    expert_id = (number + place[0] * LOCAL).astype(jnp.float32)
+    chances = []
+    product = jnp.sum(hidden * back, axis=1, keepdims=True)
+    for block in range(block_count):
+        meta = tokens[block][rows : rows + META, :].astype(jnp.float32)
+        first = jnp.where(meta[1:2, :rows] == expert_id, 1.0, 0.0)
+        second = jnp.where(meta[1:2, rows : 2 * rows] == expert_id, 1.0, 0.0)
+        pick = pick_ref[block, span, :].astype(jnp.float32)
+        chance = first * meta[0:1, :rows] + second * meta[0:1, rows : 2 * rows]
+        chances.append(jnp.sum(pick * chance, axis=1, keepdims=True))
+        spread = jnp.sum(
+            pick * product[block * CAP : (block + 1) * CAP], axis=0, keepdims=True
+        )
+        gate_grads[block, 0:1, :rows] += first * spread
+        gate_grads[block, 0:1, rows : 2 * rows] += second * spread
+    chance = jnp.concatenate(chances, axis=0)
+    back = back * chance
+    weighted = (hidden * chance).astype(jnp.bfloat16)
+    grad_gate = back * up * sigmoid * (1.0 + gate * (1.0 - sigmoid))
+    grad_up = back * silu
+    mixed = jnp.concatenate([grad_gate, grad_up], axis=1).astype(jnp.bfloat16)
+    hidden_ref[0] = weighted
+    mixed_ref[0] = mixed
+    out_part = dot_rows(weighted, down_ref[0]).astype(jnp.bfloat16)
+    out_slots[:, span, :] = out_part.reshape(block_count, CAP, width)
+    grad_part = dot_wide(mixed, wide_ref[0]).astype(jnp.bfloat16)
+    grad_slots[:, span, :] = grad_part.reshape(block_count, CAP, width)
+
+    @pl.when(number == LOCAL - 1)
+    def _():
+        for block in range(block_count):
+            pick = pick_ref[block]
+            grad_refs[block][:rows, :] = dot_tall(pick, grad_slots[block]).astype(jnp.bfloat16)
+            grad_refs[block][rows : rows + META, :] = gate_grads[block].astype(jnp.bfloat16)
+            out_refs[block][...] = dot_tall(pick, out_slots[block]).astype(jnp.bfloat16)
+
+
+def weight_grad_kernel(place, *refs):
+    slot_ref, back_ref, hidden_ref, mixed_ref = refs[:4]
+    wide_refs = refs[4:8]
+    down_refs = refs[8:12]
+    wide_sum, down_sum = refs[12:]
+    number = pl.program_id(0)
+    block_count, _, width = slot_ref.shape
+    span = pl.ds(pl.multiple_of(number * CAP, CAP), CAP)
+    rows = slot_ref[:, span, :].reshape(block_count * CAP, width)
+    wide_sum[...] = dot_tall(rows, mixed_ref[0])
+    grads = back_ref[:, span, :].reshape(block_count * CAP, width)
+    down_sum[...] = dot_tall(hidden_ref[0], grads)
+    half = wide_sum.shape[1] // 2
+    for core in range(PAIR):
+        for side in range(PAIR):
+            piece = wide_refs[core * PAIR + side]
+            depth = piece.shape[3]
+            for step in range(RING):
+                start = pl.multiple_of(owner_index(place, step, side, core) * depth, 16)
+                part = wide_sum[pl.ds(start, depth), :]
+                piece[step, 0, 0] = part[:, :half].astype(jnp.bfloat16)
+                piece[step, 1, 0] = part[:, half:].astype(jnp.bfloat16)
+            own = down_refs[core * PAIR + side]
+            deep = own.shape[1]
+            local = (place[2] ^ side) * PAIR + (place[3] ^ core)
+            part = down_sum[pl.ds(pl.multiple_of(local * deep, 16), deep), :]
+            own[0] = part.astype(jnp.bfloat16)
+
+
+def whole(shape):
+    return pl.BlockSpec(shape, lambda number, place: (0,) * len(shape))
+
+
+def by_expert(shape, axis=0):
+    return pl.BlockSpec(
+        shape,
+        lambda number, place: tuple(number if d == axis else 0 for d in range(len(shape))),
+    )
+
+
+def prepare_experts(place, grads, mixed, downs):
+    padded, width = grads[0].shape
+    rows = padded - META
+    blocks = len(grads)
+    _, _, local, depth, span = mixed[0].shape
+    deep = downs[0].shape[1]
+    model = depth * RING * PAIR * PAIR
+    slots = blocks * CAP
+    shapes = [
+        ((blocks, local * CAP, rows), jnp.bfloat16),
+        ((blocks, local * CAP, width), jnp.bfloat16),
+        ((local, slots, span), jnp.float32),
+        ((local, model, 2 * span), jnp.bfloat16),
+        ((local, deep * PAIR * PAIR, width), jnp.bfloat16),
+    ]
+    return pl.pallas_call(
+        prepare_kernel,
+        name="prepare_experts",
+        out_shape=[jax.ShapeDtypeStruct(s, d) for s, d in shapes],
+        grid_spec=pltpu.PrefetchScalarGridSpec(
+            num_scalar_prefetch=1,
+            grid=(local,),
+            in_specs=[whole(g.shape) for g in grads]
+            + [by_expert((RING, 2, 1, depth, span), 2)] * 4
+            + [by_expert((1, deep, width))] * 4,
+            out_specs=[
+                whole(shapes[0][0]),
+                whole(shapes[1][0]),
+                by_expert((1, slots, span)),
+                by_expert((1, model, 2 * span)),
+                by_expert((1, deep * PAIR * PAIR, width)),
+            ],
+        ),
+    )(place, *grads, *mixed, *downs)
+
+
+def run_experts(place, tokens, pick, wide, down, back):
+    padded, width = tokens[0].shape
+    rows = padded - META
+    blocks = len(tokens)
+    local, model, span2 = wide.shape
+    span = span2 // 2
+    slots = blocks * CAP
+    shapes = [
+        ((blocks, local * CAP, width), jnp.bfloat16),
+        ((local, slots, span), jnp.bfloat16),
+        ((local, slots, span2), jnp.bfloat16),
+    ]
+    shapes = shapes + [((padded, width), jnp.bfloat16)] * blocks
+    shapes = shapes + [((rows, width), jnp.bfloat16)] * blocks
+    results = pl.pallas_call(
+        expert_kernel,
+        name="run_experts",
+        out_shape=[jax.ShapeDtypeStruct(s, d) for s, d in shapes],
+        grid_spec=pltpu.PrefetchScalarGridSpec(
+            num_scalar_prefetch=1,
+            grid=(local,),
+            in_specs=[whole(t.shape) for t in tokens]
+            + [
+                whole(pick.shape),
+                by_expert((1, model, span2)),
+                by_expert((1, span, width)),
+                by_expert((1, slots, span)),
+            ],
+            out_specs=[
+                whole(shapes[0][0]),
+                by_expert((1, slots, span)),
+                by_expert((1, slots, span2)),
+            ]
+            + [whole(s) for s, _ in shapes[3:]],
+            scratch_shapes=[
+                pltpu.VMEM((blocks, local * CAP, width), jnp.bfloat16),
+                pltpu.VMEM((blocks, local * CAP, width), jnp.bfloat16),
+                pltpu.VMEM((blocks, META, width), jnp.float32),
+            ],
+        ),
+    )(place, *tokens, pick, wide, down, back)
+    return results[:3], results[3 : 3 + blocks], results[3 + blocks :]
+
+
+def weight_grads(place, slots, backs, hidden, mixed):
+    blocks, total, width = slots.shape
+    local, rows, span = hidden.shape
+    depth = width // (RING * PAIR * PAIR)
+    deep = span // (PAIR * PAIR)
+    wide_shape = (RING, 2, local, depth, span)
+    down_shape = (local, deep, width)
+    results = pl.pallas_call(
+        weight_grad_kernel,
+        name="weight_grads",
+        out_shape=[jax.ShapeDtypeStruct(wide_shape, jnp.bfloat16)] * 4
+        + [jax.ShapeDtypeStruct(down_shape, jnp.bfloat16)] * 4,
+        grid_spec=pltpu.PrefetchScalarGridSpec(
+            num_scalar_prefetch=1,
+            grid=(local,),
+            in_specs=[
+                whole(slots.shape),
+                whole(backs.shape),
+                by_expert((1, rows, span)),
+                by_expert((1, rows, 2 * span)),
+            ],
+            out_specs=[by_expert((RING, 2, 1, depth, span), 2)] * 4
+            + [by_expert((1, deep, width))] * 4,
+            scratch_shapes=[
+                pltpu.VMEM((width, 2 * span), jnp.float32),
+                pltpu.VMEM((span, width), jnp.float32),
+            ],
+        ),
+    )(place, slots, backs, hidden, mixed)
+    return results[:4], results[4:]
+
+
+def add_low(left, right):
+    return (left.astype(jnp.float32) + right.astype(jnp.float32)).astype(jnp.bfloat16)
+
+
+def exchange_expert_weights(gate_weight, up_weight, down_weight, z_place):
+    span = gate_weight.shape[2] // RING
+    pieces = []
+    for step in range(RING):
+        start = lax.rem(z_place + step, RING) * span
+        piece = jnp.stack(
+            [
+                lax.dynamic_slice_in_dim(gate_weight, start, span, 2),
+                lax.dynamic_slice_in_dim(up_weight, start, span, 2),
+            ]
+        )
+        pieces.append(along_z(piece, step) if step else piece)
+    own = jnp.stack(pieces)
+    other = across_y(own)
+    mixed = [own, other, across_core(own), across_core(other)]
+    down_other = across_y(down_weight)
+    downs = [down_weight, down_other, across_core(down_weight), across_core(down_other)]
+    return mixed, downs
+
+
+def reduce_expert_grads(mixed, downs, z_place):
+    near = add_low(mixed[0], across_core(mixed[2]))
+    far = add_low(mixed[1], across_core(mixed[3]))
+    mine = add_low(near, across_y(far))
+    parts = [mine[0]] + [along_z(mine[step], -step) for step in range(1, RING)]
+    columns = []
+    for column in range(RING):
+        choice = lax.rem(column - z_place + RING, RING)
+        chosen = parts[0]
+        for step in range(1, RING):
+            chosen = jnp.where(choice == step, parts[step], chosen)
+        columns.append(chosen)
+    both = jnp.concatenate(columns, axis=-1).astype(jnp.float32)
+    near = add_low(downs[0], across_core(downs[2]))
+    far = add_low(downs[1], across_core(downs[3]))
+    down = near.astype(jnp.float32) + across_y(far).astype(jnp.float32)
+    return both[0], both[1], down
+
+
+def body_split(
+    tokens,
+    segment_ids,
+    routes,
+    earlier_logits,
+    out_cotangent,
+    query_weight,
+    key_weight,
+    value_weight,
+    output_weight,
+    router_weight,
+    const_vectors,
+    attn_gain,
+    moe_gain,
+    gate_weight,
+    up_weight,
+    down_weight,
+):
+    _, pos_count, model_width = tokens.shape
+    tokens, segment_row, routes = tokens[0], segment_ids[0], routes[0]
+    earlier_logits, cotangent_low = earlier_logits[0], out_cotangent[0]
+    x_place = lax.axis_index("expert")
+    shard_place = lax.axis_index("shard")
+    z_place = shard_place // (PAIR * PAIR)
+    y_place = lax.rem(shard_place // PAIR, PAIR)
+    core_place = lax.rem(shard_place, PAIR)
+    order = jnp.arange(4, dtype=jnp.int32)
+    place = jnp.where(
+        order == 0,
+        x_place,
+        jnp.where(order == 1, z_place, jnp.where(order == 2, y_place, core_place)),
+    ).astype(jnp.int32)
+    choices = router_weight.shape[1]
+    consts = const_vectors.shape[1]
+    small_count = choices + consts + 2
+    small = jnp.concatenate(
+        [router_weight, const_vectors, attn_gain[:, None], moe_gain[:, None]], axis=1
+    )
+    small = jnp.pad(small, ((0, 0), (0, 128 - small_count)))
+    packed = jnp.concatenate(
+        [query_weight, key_weight, value_weight, output_weight, small], axis=1
+    )
+    gathered = lax.all_gather(packed, "shard", axis=0, tiled=True)
+    other_tokens = across_x(tokens)
+    routes_low = routes.astype(jnp.bfloat16)
+    route_rows = [routes_low[:, 0], routes_low[:, 1]]
+    zero_rows = [jnp.zeros_like(route_rows[0])] * 2
+    cotangent_blocks = gather_rows(
+        jnp.concatenate([cotangent_low, meta_rows(zero_rows + route_rows, model_width)], axis=0)
+    )
+    mixed_pieces, down_pieces = exchange_expert_weights(
+        gate_weight, up_weight, down_weight, z_place
+    )
+    pick, back_slots, back_hidden, wide_full, down_full = prepare_experts(
+        place, cotangent_blocks, mixed_pieces, down_pieces
+    )
+
+    joint = 3 * model_width
+    joint_weight = gathered[:, :joint]
+    output_wide = gathered[:, joint : joint + model_width]
+    tail = gathered[:, joint + model_width :].astype(jnp.float32)
+    router_low = gathered[:, joint + model_width : joint + model_width + choices]
+    router_wide = tail[:, :choices]
+    const_wide = tail[:, choices : choices + consts].T
+    gain_attn = tail[:, choices + consts]
+    gain_moe = tail[:, choices + consts + 1]
+
+    offset = x_place * pos_count
+    width_block = math.gcd(pos_count, 128)
+    block_count = (x_place + 1) * (pos_count // width_block)
+    first_tokens = jnp.where(x_place == 0, tokens, other_tokens)
+    second_tokens = jnp.where(x_place == 0, other_tokens, tokens)
+    all_wide = jnp.concatenate([first_tokens, second_tokens], axis=0).astype(jnp.float32)
+    scaled_all, _ = rms_parts(all_wide)
+    normed_all = (scaled_all * gain_attn).astype(jnp.bfloat16)
+    tokens_wide = tokens.astype(jnp.float32)
+    scaled_one, inverse_one = rms_parts(tokens_wide)
+    normed_own = (scaled_one * gain_attn).astype(jnp.bfloat16)
+    positions = offset + jnp.arange(pos_count, dtype=jnp.int32)
+    all_positions = jnp.arange(PAIR * pos_count, dtype=jnp.int32)
+    query_rot = rotary(dot_rows(normed_own, joint_weight[:, :model_width]), positions, 1.0)
+    query_rot = query_rot.astype(jnp.bfloat16)
+    key_value = dot_rows(normed_all, joint_weight[:, model_width:])
+    keys_all = rotary(key_value[:, :model_width], all_positions, 1.0).astype(jnp.bfloat16)
+    values_all = key_value[:, model_width:].astype(jnp.bfloat16)
+    attention_output, log_total = attend_forward(
+        query_rot, keys_all, values_all, segment_row, offset, block_count, width_block
+    )
+    attention_low = attention_output.astype(jnp.bfloat16)
+    middle = tokens_wide + dot_rows(attention_low, output_wide)
+    scaled_two, inverse_two = rms_parts(middle)
+    normed_two = scaled_two * gain_moe
+    normed_low = normed_two.astype(jnp.bfloat16)
+    router_logits = dot_rows(normed_low, router_low) + earlier_logits
+    choice_ids = jnp.arange(choices, dtype=jnp.int32)
+    one_hot = (routes[..., None] == choice_ids).astype(jnp.float32)
+    chosen = jnp.sum(one_hot * router_logits[:, None, :], axis=-1)
+    gate_probs = jax.nn.softmax(chosen, axis=-1)
+    probs_low = gate_probs.astype(jnp.bfloat16)
+    token_blocks = gather_rows(
+        jnp.concatenate(
+            [
+                normed_low,
+                meta_rows([probs_low[:, 0], probs_low[:, 1]] + route_rows, model_width),
+            ],
+            axis=0,
+        )
+    )
+    (token_slots, hidden, mixed), grad_parts, out_parts = run_experts(
+        place, token_blocks, pick, wide_full, down_full, back_hidden
+    )
+    grad_total = reduce_rows(grad_parts)
+    wide_grads, down_grads = weight_grads(place, token_slots, back_slots, hidden, mixed)
+    out_total = reduce_rows(out_parts)
+    gate_grad, up_grad, down_grad = reduce_expert_grads(wide_grads, down_grads, z_place)
+
+    cotangent = cotangent_low.astype(jnp.float32)
+    copies = jnp.sum(one_hot[..., EXPERTS + 1] * gate_probs, axis=-1)[:, None]
+    const_probs = jnp.sum(one_hot[..., EXPERTS + 2 :] * gate_probs[..., None], axis=1)
+    const_rows = sum(const_probs[:, i : i + 1] * const_wide[i : i + 1] for i in range(consts))
+    layer_out = middle + out_total + copies * normed_two + const_rows
+    copy_dot = jnp.sum(cotangent * normed_two, axis=-1)
+    const_dot = jnp.stack(
+        [jnp.sum(cotangent * const_wide[i], axis=-1) for i in range(consts)], axis=-1
+    )
+    grad_rows = grad_total[:pos_count]
+    expert_dot = jnp.stack(
+        [grad_total[pos_count, i * pos_count : (i + 1) * pos_count] for i in range(2)], axis=-1
+    )
+    grad_gates = (
+        expert_dot
+        + one_hot[..., EXPERTS + 1] * copy_dot[:, None]
+        + jnp.sum(one_hot[..., EXPERTS + 2 :] * const_dot[:, None, :], axis=-1)
+    )
+    grad_chosen = gate_probs * (
+        grad_gates - jnp.sum(gate_probs * grad_gates, axis=-1, keepdims=True)
+    )
+    prior_logits_gradient = jnp.sum(one_hot * grad_chosen[..., None], axis=1)
+    highest = lax.Precision.HIGHEST
+    grad_normed_two = (
+        grad_rows
+        + copies * cotangent
+        + jnp.einsum("wk,ok->wo", prior_logits_gradient, router_wide, precision=highest)
+    )
+    router_part = jnp.einsum(
+        "rx,rb->xb", normed_low.astype(jnp.float32), prior_logits_gradient, precision=highest
+    )
+    const_part = jnp.einsum("rx,rb->xb", cotangent, const_probs, precision=highest)
+    moe_gain_part = jnp.sum(grad_normed_two * scaled_two, axis=0)
+    grad_middle = cotangent + rms_back(grad_normed_two * gain_moe, middle, inverse_two)
+    grad_projected = grad_middle.astype(jnp.bfloat16)
+    output_part = dot_tall(attention_low, grad_projected)
+    grad_attended = dot_wide(grad_projected, output_wide).astype(jnp.bfloat16)
+    delta_sum = jnp.transpose(
+        jnp.sum(
+            (grad_attended.astype(jnp.float32) * attention_output).reshape(pos_count, HEADS, -1),
+            axis=-1,
+        )
+    )
+    grad_query_rot, grad_keys, grad_values = attend_backward(
+        query_rot,
+        keys_all,
+        values_all,
+        segment_row,
+        log_total,
+        delta_sum,
+        grad_attended,
+        offset,
+        block_count,
+        width_block,
+    )
+    grad_query = rotary(grad_query_rot, positions, -1.0).astype(jnp.bfloat16)
+    grad_key = rotary(grad_keys, all_positions, -1.0).astype(jnp.bfloat16)
+    grad_value = grad_values.astype(jnp.bfloat16)
+    grad_key_value = jnp.concatenate([grad_key, grad_value], axis=1)
+    grad_normed_all = dot_wide(grad_key_value, joint_weight[:, model_width:])
+    first_grad = grad_normed_all[:pos_count]
+    shared = lax.ppermute(first_grad.astype(jnp.bfloat16), "expert", [(1, 0)])
+    own_grad = jnp.where(x_place == 0, first_grad, grad_normed_all[pos_count:])
+    grad_normed_one = (
+        dot_wide(grad_query, joint_weight[:, :model_width]) + own_grad + shared.astype(jnp.float32)
+    )
+    query_part = dot_tall(normed_own, grad_query)
+    key_value_part = dot_tall(normed_all, grad_key_value)
+    attn_gain_part = jnp.sum(grad_normed_one * scaled_one, axis=0)
+    tokens_grad = grad_middle + rms_back(grad_normed_one * gain_attn, tokens_wide, inverse_one)
+    small_part = jnp.concatenate(
+        [router_part, const_part, attn_gain_part[:, None], moe_gain_part[:, None]], axis=1
+    )
+    small_part = jnp.pad(small_part, ((0, 0), (0, 128 - small_count)))
+    output_sum = lax.psum_scatter(
+        output_part.astype(jnp.bfloat16), "shard", scatter_dimension=0, tiled=True
+    )
+    packed_part = jnp.concatenate([query_part, key_value_part, small_part], axis=1)
+    packed_sum = lax.psum_scatter(
+        packed_part.astype(jnp.bfloat16), "shard", scatter_dimension=0, tiled=True
+    )
+    output_grad = output_sum.astype(jnp.float32) + across_x(output_sum).astype(jnp.float32)
+    packed_grad = packed_sum.astype(jnp.float32) + across_x(packed_sum).astype(jnp.float32)
+    small_grad = packed_grad[:, joint:]
+    return (
+        layer_out.astype(jnp.bfloat16)[None],
+        tokens_grad[None],
+        prior_logits_gradient[None],
+        packed_grad[:, :model_width],
+        packed_grad[:, model_width : 2 * model_width],
+        packed_grad[:, 2 * model_width : joint],
+        output_grad,
+        small_grad[:, :choices],
+        small_grad[:, choices : choices + consts],
+        small_grad[:, choices + consts],
+        small_grad[:, choices + consts + 1],
+        gate_grad,
+        up_grad,
+        down_grad,
+    )
+
+
 def solution(mesh):
     in_specs = (
         P("shard", "expert", None),
@@ -557,4 +1166,6 @@
         P("expert", "shard", None),
         P("expert", "shard", None),
     )
-    return jax.shard_map(body, mesh=mesh, in_specs=in_specs, out_specs=out_specs, check_vma=False)
+    divided = mesh.shape["expert"] == PAIR and mesh.shape["shard"] == RING * PAIR * PAIR
+    chosen = body_split if divided else body
+    return jax.shard_map(chosen, mesh=mesh, in_specs=in_specs, out_specs=out_specs, check_vma=False)

time: 1450 us -> 568 us (0.39)
  the two profiles are of different devices: /device:TPU:0 before, /device:TPU:10 now
where the time goes in v1:
time: 568 us; the launch traced here: 559 us
  waiting for transfers between devices  295 us (52%)
  local copies, waits for them, and re-layouts  55.4 us (10%)
  other arithmetic  52 us (9%)
  Pallas kernels  50.1 us (9%)
  starting transfers between devices  46.6 us (8%)
  matrix products  43.2 us (8%)
  between operations  15.3 us (3%)
    ppermute x18, waiting for transfers between devices, along_z(): return lax.ppermute(values, 'shard', z_pairs(step))  107 us
    ppermute x4, waiting for transfers between devices, across_y(): lax.ppermute(values, 'shard', [(s, s ^ PAIR) for s in range(RING * PAIR *...  106 us
    ppermute x19, waiting for transfers between devices, across_x(): return lax.ppermute(values, 'expert', [(0, 1), (1, 0)])  78.4 us
    ppermute x18, starting transfers between devices, along_z(): return lax.ppermute(values, 'shard', z_pairs(step))  29.3 us
    pallas_call x1, Pallas kernels, run_experts(): pl.pallas_call(expert_kernel, name='run_experts', out_shape=[jax.ShapeDty...  22.8 us
    pallas_call x1, Pallas kernels, prepare_experts(): pl.pallas_call(prepare_kernel, name='prepare_experts', out_shape=[jax.Sha...  14.5 us
    pallas_call x1, Pallas kernels, weight_grads(): pl.pallas_call(weight_grad_kernel, name='weight_grads', out_shape=[jax.Sh...  12.8 us
  transfers between devices with their start and end apart: 53, of which 29 were waited for; matrix products, arithmetic and copies ran while one was open for 24% of the time, Pallas kernels for 5%

profile of v1, /device:TPU:10, one launch (start us, length us, event | category | flops | bytes accessed | tf_op | source)
XLA Modules:
  0.0 558.5 jit_solution(1750991623831377226)
XLA Ops:
  20.7 24.7 %collective-permute-done.15 = bf16[2,4,48,512]{3,2,1,0:T(8,128)(2,1)S(1)} collective-permute-done((bf16[2,4,48,512]{3,2,1,0:T(8,128)(2,1)S(1)}, bf16[2,4,48,512]{3,2,1,0:T(8,128)(2,1)S(1)}, u32[]{:S(2)}, u32[]{:S(2)}) %collective-permute-start.15) | collective-permute-done | bytes 393248 | tf_op jit(solution)/shard_map/ppermute | solution.py:543
  45.7 15.7 %collective-permute-done.16 = bf16[2,4,48,512]{3,2,1,0:T(8,128)(2,1)S(1)} collective-permute-done((bf16[2,4,48,512]{3,2,1,0:T(8,128)(2,1)S(1)}, bf16[2,4,48,512]{3,2,1,0:T(8,128)(2,1)S(1)}, u32[]{:S(2)}, u32[]{:S(2)}) %collective-permute-start.16) | collective-permute-done | bytes 393248 | tf_op jit(solution)/shard_map/ppermute | solution.py:543
  67.8 43.4 %collective-permute-done.18.refs_9_ = bf16[4,2,4,48,512]{4,3,2,1,0:T(8,128)(2,1)} collective-permute-done((bf16[4,2,4,48,512]{4,3,2,1,0:T(8,128)(2,1)}, bf16[4,2,4,48,512]{4,3,2,1,0:T(8,128)(2,1)}, u32[]{:S(2)}, u32[]{:S(2)}) %collective-permute-start.18) | collective-permute-done | bytes 1572896 | tf_op jit(solution)/shard_map/ppermute | solution.py:547
  123.2 7.0 %while.39 = (s32[]{:T(128)}, f32[12,256]{1,0:T(8,128)S(1)}, f32[12,256]{1,0:T(8,128)S(1)}, s32[]{:T(128)}, s32[512]{0:T(512)}, /*index=5*/s32[256]{0:T(256)S(1)}...) while((s32[]{:T(128)}, f32[12,256]{1,0:T(8,128)S(1)}, ...), condition=%wide.region_5.6_spmd.clone, body=%wide.region_2.5_spmd.clone.sunk | while | flops 52795780 | bytes 4392635 | solution.py:88
  131.4 10.3 %while.40 = (s32[]{:T(128)}, f32[256,12,64]{0,2,1:T(8,128)S(1)}, s32[]{:T(128)}, bf16[512,768]{0,1:T(8,128)(2,1)}, s32[512]{0:T(512)}, /*index=5*/s32[256]{0:T(2...) while((s32[]{:T(128)}, f32[256,12,64]{0,2,1:T(8,128)S(1)}, ...), condition=%wide.region_7.8_spmd.clone, body=%wide.region_6.7_spmd.clone.sunk | while | flops 102531464 | bytes 3229379 | solution.py:107
  160.9 6.8 %collective-permute-done.8.refs_1_ = bf16[272,768]{1,0:T(8,128)(2,1)} collective-permute-done((bf16[272,768]{1,0:T(8,128)(2,1)}, bf16[272,768]{1,0:T(8,128)(2,1)}, u32[]{:S(2)}, u32[]{:S(2)}) %collective-permute-start.8) | collective-permute-done | bytes 417824 | tf_op jit(solution)/shard_map/ppermute | solution.py:543
  169.2 7.5 %collective-permute-done.1.refs_1_ = bf16[272,768]{1,0:T(8,128)(2,1)} collective-permute-done((bf16[272,768]{1,0:T(8,128)(2,1)}, bf16[272,768]{1,0:T(8,128)(2,1)}, u32[]{:S(2)}, u32[]{:S(2)}) %collective-permute-start.1) | collective-permute-done | bytes 417824 | tf_op jit(solution)/shard_map/ppermute | solution.py:543
  178.1 7.4 %collective-permute-done.9.refs_2_ = bf16[272,768]{1,0:T(8,128)(2,1)S(1)} collective-permute-done((bf16[272,768]{1,0:T(8,128)(2,1)}, bf16[272,768]{1,0:T(8,128)(2,1)S(1)}, u32[]{:S(2)}, u32[]{:S(2)}) %collective-permute-start.9) | collective-permute-done | bytes 417824 | tf_op jit(solution)/shard_map/ppermute | solution.py:543
  189.0 5.5 collective-permute-done.2.refs_2_
  196.2 7.3 %collective-permute-done.10.refs_3_ = bf16[272,768]{1,0:T(8,128)(2,1)} collective-permute-done((bf16[272,768]{1,0:T(8,128)(2,1)S(1)}, bf16[272,768]{1,0:T(8,128)(2,1)}, u32[]{:S(2)}, u32[]{:S(2)}) %collective-permute-start.10) | collective-permute-done | bytes 417824 | tf_op jit(solution)/shard_map/ppermute | solution.py:543
  212.5 14.2 %collective-permute-done.14.refs_7_ = bf16[272,768]{1,0:T(8,128)(2,1)} collective-permute-done((bf16[272,768]{1,0:T(8,128)(2,1)}, bf16[272,768]{1,0:T(8,128)(2,1)}, u32[]{:S(2)}, u32[]{:S(2)}) %collective-permute-start.14) | collective-permute-done | bytes 417824 | tf_op jit(solution)/shard_map/ppermute | solution.py:555
  226.7 14.5 %prepare_experts.1 = (bf16[8,256,256]{2,1,0:T(8,128)(2,1)}, bf16[8,256,768]{2,1,0:T(8,128)(2,1)}, f32[4,512,512]{2,1,0:T(8,128)}, bf16[4,768,1024]{2,1,0:T(8,128)(2,1)}, bf16[4,512,768]{2,1,0:T(8,128)(2,1)}) custom-call(s32[4]{0:T(128)} %compare_select_fusion.2.place, bf16[272,768]{1,0:T(8,128)(2,1)} %fusion.52.refs_0_, ...), custom_call_target="tpu_custom_call" | custom-call | tf_op jit(solution)/shard_map/prepare_experts/pallas_call | solution.py:776
  244.6 7.0 %collective-permute-done.7.refs_7_ = bf16[272,768]{1,0:T(8,128)(2,1)} collective-permute-done((bf16[272,768]{1,0:T(8,128)(2,1)}, bf16[272,768]{1,0:T(8,128)(2,1)}, u32[]{:S(2)}, u32[]{:S(2)}) %collective-permute-start.7) | collective-permute-done | bytes 417824 | tf_op jit(solution)/shard_map/ppermute | solution.py:555
  251.6 22.8 %run_experts.1 = (bf16[8,256,768]{2,1,0:T(8,128)(2,1)}, bf16[4,512,512]{2,1,0:T(8,128)(2,1)}, bf16[4,512,1024]{2,1,0:T(8,128)(2,1)}, bf16[272,768]{1,0:T(8,128)(...) custom-call(s32[4]{0:T(128)} %compare_select_fusion.2.place, ...), custom_call_target="tpu_custom_call" | custom-call | tf_op jit(solution)/shard_map/run_experts/pallas_call | solution.py:811
  278.1 9.1 %collective-permute-done.34 = bf16[272,768]{1,0:T(8,128)(2,1)S(1)} collective-permute-done((bf16[272,768]{1,0:T(8,128)(2,1)}, bf16[272,768]{1,0:T(8,128)(2,1)S(1)}, u32[]{:S(2)}, u32[]{:S(2)}) %collective-permute-start.34) | collective-permute-done | bytes 417824 | tf_op jit(solution)/shard_map/ppermute | solution.py:555
  314.7 7.2 %collective-permute-done.32 = bf16[272,768]{1,0:T(8,128)(2,1)S(1)} collective-permute-done((bf16[272,768]{1,0:T(8,128)(2,1)}, bf16[272,768]{1,0:T(8,128)(2,1)S(1)}, u32[]{:S(2)}, u32[]{:S(2)}) %collective-permute-start.32) | collective-permute-done | bytes 417824 | tf_op jit(solution)/shard_map/ppermute | solution.py:555
  323.7 6.7 %collective-permute-done.25 = bf16[256,768]{1,0:T(8,128)(2,1)S(1)} collective-permute-done((bf16[256,768]{1,0:T(8,128)(2,1)S(1)}, bf16[256,768]{1,0:T(8,128)(2,1)S(1)}, u32[]{:S(2)}, u32[]{:S(2)}) %collective-permute-start.25) | collective-permute-done | bytes 393248 | tf_op jit(solution)/shard_map/ppermute | solution.py:555
  332.1 7.3 %collective-permute-done.31 = bf16[272,768]{1,0:T(8,128)(2,1)S(1)} collective-permute-done((bf16[272,768]{1,0:T(8,128)(2,1)S(1)}, bf16[272,768]{1,0:T(8,128)(2,1)S(1)}, u32[]{:S(2)}, u32[]{:S(2)}) %collective-permute-start.31) | collective-permute-done | bytes 417824 | tf_op jit(solution)/shard_map/ppermute | solution.py:555
  354.8 27.0 %while.41 = (s32[]{:T(128)}, f32[256,12,64]{0,2,1:T(8,128)S(1)}, f32[512,768]{0,1:T(8,128)}, bf16[512,768]{0,1:T(8,128)(2,1)}, s32[]{:T(128)}, /*index=5*/bf16[5...) while((s32[]{:T(128)}, f32[256,12,64]{0,2,1:T(8,128)S(1)}, ...), condition=%wide.region_23.24_spmd.clone, body=%wide.region_22.23_spmd.clone.sunk | while | flops 255099264 | bytes 13465323 | solution.py:179
  405.5 12.8 %weight_grads.1 = (bf16[4,2,4,48,512]{4,3,2,1,0:T(8,128)(2,1)}, bf16[4,2,4,48,512]{4,3,2,1,0:T(8,128)(2,1)}, bf16[4,2,4,48,512]{4,3,2,1,0:T(8,128)(2,1)}, bf16[4...) custom-call(s32[4]{0:T(128)} %compare_select_fusion.2.place, ...), custom_call_target="tpu_custom_call" | custom-call | tf_op jit(solution)/shard_map/weight_grads/pallas_call | solution.py:848
  429.0 63.0 %collective-permute-done.49 = bf16[4,128,768]{2,1,0:T(8,128)(2,1)} collective-permute-done((bf16[4,128,768]{2,1,0:T(8,128)(2,1)}, bf16[4,128,768]{2,1,0:T(8,128)(2,1)}, u32[]{:S(2)}, u32[]{:S(2)}) %collective-permute-start.49) | collective-permute-done | bytes 786464 | tf_op jit(solution)/shard_map/ppermute | solution.py:547
  511.8 17.0 %collective-permute-done.44 = bf16[2,4,48,512]{3,2,1,0:T(8,128)(2,1)} collective-permute-done((bf16[2,4,48,512]{3,2,1,0:T(8,128)(2,1)}, bf16[2,4,48,512]{3,2,1,0:T(8,128)(2,1)}, u32[]{:S(2)}, u32[]{:S(2)}) %collective-permute-start.44) | collective-permute-done | bytes 393248 | tf_op jit(solution)/shard_map/ppermute | solution.py:543
  528.9 6.7 %collective-permute-done.45 = bf16[2,4,48,512]{3,2,1,0:T(8,128)(2,1)} collective-permute-done((bf16[2,4,48,512]{3,2,1,0:T(8,128)(2,1)}, bf16[2,4,48,512]{3,2,1,0:T(8,128)(2,1)}, u32[]{:S(2)}, u32[]{:S(2)}) %collective-permute-start.45) | collective-permute-done | bytes 393248 | tf_op jit(solution)/shard_map/ppermute | solution.py:543
  542.7 5.9 %collective-permute-done.39 = bf16[48,2432]{1,0:T(8,128)(2,1)S(1)} collective-permute-done((bf16[48,2432]{1,0:T(8,128)(2,1)}, bf16[48,2432]{1,0:T(8,128)(2,1)S(1)}, u32[]{:S(2)}, u32[]{:S(2)}) %collective-permute-start.39) | collective-permute-done | bytes 233504 | tf_op jit(solution)/shard_map/ppermute | solution.py:555
  (457 shorter events, 229.9 us)
Async XLA Ops:
  7.2 104.0 %all-gather.2.cloned.1.call-start = ((), (), s32[]{:S(2)}) async-start(), calls=%async_computation.2 | async-start | bytes 5222400 | tf_op jit(solution)/shard_map/all_gather | solution.py:958
  12.5 494.1 %reduce-scatter.5.cloned.1.call-start = ((), (), s32[]{:S(2)}) async-start(), calls=%async_computation.4 | async-start | bytes 1253376 | tf_op jit(solution)/shard_map/reduce_scatter | solution.py:1106
  12.5 146.9 %collective-permute-start.21 = (bf16[4,128,768]{2,1,0:T(8,128)(2,1)}, bf16[4,128,768]{2,1,0:T(8,128)(2,1)}, u32[]{:S(2)}, u32[]{:S(2)}) collective-permute-start(bf16[4,128,768]{2,1,0:T(8,128)(2,1)} %refs_12_.1), channel_id=1, source_target_pairs={{0,2},{1,3},{2,0},{3,1},{4,6},{5,7},{6,4},{7,5},{8,10},{9,11},{10,... | collective-permute-start | bytes 2359304 | tf_op jit(solution)/shard_map/ppermute | solution.py:547
  14.1 146.8 %collective-permute-start.22 = (bf16[4,128,768]{2,1,0:T(8,128)(2,1)}, bf16[4,128,768]{2,1,0:T(8,128)(2,1)}, u32[]{:S(2)}, u32[]{:S(2)}) collective-permute-start(bf16[4,128,768]{2,1,0:T(8,128)(2,1)} %refs_12_.1), channel_id=1, source_target_pairs={{0,1},{1,0},{2,3},{3,2},{4,5},{5,4},{6,7},{7,6},{8,9},{9,8},{10,11... | collective-permute-start | bytes 2359304 | tf_op jit(solution)/shard_map/ppermute | solution.py:551
  15.6 29.9 %collective-permute-start.15 = (bf16[2,4,48,512]{3,2,1,0:T(8,128)(2,1)S(1)}, bf16[2,4,48,512]{3,2,1,0:T(8,128)(2,1)S(1)}, u32[]{:S(2)}, u32[]{:S(2)}) collective-permute-start(bf16[2,4,48,512]{3,2,1,0:T(8,128)(2,1)S(1)} %pad_maximum_fusion.8), channel_id=1, source_target_pairs={{0,4},{1,5},{2,6},{3,7},{4,8},{5,9},{6,10},{7,11},{8,12},{9,13},{1... | collective-permute-start | bytes 1179656 | tf_op jit(solution)/shard_map/ppermute | solution.py:543
  17.2 44.2 %collective-permute-start.16 = (bf16[2,4,48,512]{3,2,1,0:T(8,128)(2,1)S(1)}, bf16[2,4,48,512]{3,2,1,0:T(8,128)(2,1)S(1)}, u32[]{:S(2)}, u32[]{:S(2)}) collective-permute-start(bf16[2,4,48,512]{3,2,1,0:T(8,128)(2,1)S(1)} %pad_maximum_fusion.9), channel_id=1, source_target_pairs={{0,8},{1,9},{2,10},{3,11},{4,12},{5,13},{6,14},{7,15},{8,0},{9,1},... | collective-permute-start | bytes 1179656 | tf_op jit(solution)/shard_map/ppermute | solution.py:543
  18.6 44.7 %collective-permute-start.17 = (bf16[2,4,48,512]{3,2,1,0:T(8,128)(2,1)S(1)}, bf16[2,4,48,512]{3,2,1,0:T(8,128)(2,1)S(1)}, u32[]{:S(2)}, u32[]{:S(2)}) collective-permute-start(bf16[2,4,48,512]{3,2,1,0:T(8,128)(2,1)S(1)} %pad_maximum_fusion.10), channel_id=1, source_target_pairs={{0,12},{1,13},{2,14},{3,15},{4,0},{5,1},{6,2},{7,3},{8,4},{9,5},{1... | collective-permute-start | bytes 1179656 | tf_op jit(solution)/shard_map/ppermute | solution.py:543
  64.6 46.6 %collective-permute-start.18 = (bf16[4,2,4,48,512]{4,3,2,1,0:T(8,128)(2,1)}, bf16[4,2,4,48,512]{4,3,2,1,0:T(8,128)(2,1)}, u32[]{:S(2)}, u32[]{:S(2)}) collective-permute-start(bf16[4,2,4,48,512]{4,3,2,1,0:T(8,128)(2,1)} %pad_maximum_fusion.refs_8_), channel_id=1, source_target_pairs={{0,2},{1,3},{2,0},{3,1},{4,6},{5,7},{6,4},{7,5},{8,10},{9,11},{10,... | collective-permute-start | bytes 4718600 | tf_op jit(solution)/shard_map/ppermute | solution.py:547
  67.4 119.5 %collective-permute-start.19 = (bf16[4,2,4,48,512]{4,3,2,1,0:T(8,128)(2,1)}, bf16[4,2,4,48,512]{4,3,2,1,0:T(8,128)(2,1)}, u32[]{:S(2)}, u32[]{:S(2)}) collective-permute-start(bf16[4,2,4,48,512]{4,3,2,1,0:T(8,128)(2,1)} %pad_maximum_fusion.refs_8_), channel_id=1, source_target_pairs={{0,1},{1,0},{2,3},{3,2},{4,5},{5,4},{6,7},{7,6},{8,9},{9,8},{10,11... | collective-permute-start | bytes 4718600 | tf_op jit(solution)/shard_map/ppermute | solution.py:551
  111.1 75.8 %collective-permute-start.20 = (bf16[4,2,4,48,512]{4,3,2,1,0:T(8,128)(2,1)}, bf16[4,2,4,48,512]{4,3,2,1,0:T(8,128)(2,1)}, u32[]{:S(2)}, u32[]{:S(2)}) collective-permute-start(bf16[4,2,4,48,512]{4,3,2,1,0:T(8,128)(2,1)} %collective-permute-done.18.refs_9_), channel_id=1, source_target_pairs={{0,1},{1,0},{2,3},{3,2},{4,5},{5,4},{6,7},{7,6},{8,9},{9,8},{10,11... | collective-permute-start | bytes 4718600 | tf_op jit(solution)/shard_map/ppermute | solution.py:551
  196.2 44.9 %collective-permute-start.4 = (bf16[272,768]{1,0:T(8,128)(2,1)}, bf16[272,768]{1,0:T(8,128)(2,1)}, u32[]{:S(2)}, u32[]{:S(2)}) collective-permute-start(bf16[272,768]{1,0:T(8,128)(2,1)} %fusion.51.refs_0_), channel_id=1, source_target_pairs={{0,16},{16,0},{1,17},{17,1},{2,18},{18,2},{3,19},{19,3},{4,20},{20... | collective-permute-start | bytes 1253384 | tf_op jit(solution)/shard_map/ppermute | solution.py:555
  203.5 37.6 %collective-permute-start.5 = (bf16[272,768]{1,0:T(8,128)(2,1)}, bf16[272,768]{1,0:T(8,128)(2,1)}, u32[]{:S(2)}, u32[]{:S(2)}) collective-permute-start(bf16[272,768]{1,0:T(8,128)(2,1)} %collective-permute-done.1.refs_1_), channel_id=1, source_target_pairs={{0,16},{16,0},{1,17},{17,1},{2,18},{18,2},{3,19},{19,3},{4,20},{20... | collective-permute-start | bytes 1253384 | tf_op jit(solution)/shard_map/ppermute | solution.py:555
  208.6 35.9 %collective-permute-start.6 = (bf16[272,768]{1,0:T(8,128)(2,1)}, bf16[272,768]{1,0:T(8,128)(2,1)}, u32[]{:S(2)}, u32[]{:S(2)}) collective-permute-start(bf16[272,768]{1,0:T(8,128)(2,1)} %collective-permute-done.2.refs_2_), channel_id=1, source_target_pairs={{0,16},{16,0},{1,17},{17,1},{2,18},{18,2},{3,19},{19,3},{4,20},{20... | collective-permute-start | bytes 1253384 | tf_op jit(solution)/shard_map/ppermute | solution.py:555
  212.0 39.6 %collective-permute-start.7 = (bf16[272,768]{1,0:T(8,128)(2,1)}, bf16[272,768]{1,0:T(8,128)(2,1)}, u32[]{:S(2)}, u32[]{:S(2)}) collective-permute-start(bf16[272,768]{1,0:T(8,128)(2,1)} %collective-permute-done.3.refs_3_), channel_id=1, source_target_pairs={{0,16},{16,0},{1,17},{17,1},{2,18},{18,2},{3,19},{19,3},{4,20},{20... | collective-permute-start | bytes 1253384 | tf_op jit(solution)/shard_map/ppermute | solution.py:555
  277.8 26.9 %collective-permute-start.33 = (bf16[272,768]{1,0:T(8,128)(2,1)}, bf16[272,768]{1,0:T(8,128)(2,1)}, u32[]{:S(2)}, u32[]{:S(2)}) collective-permute-start(bf16[272,768]{1,0:T(8,128)(2,1)} %get-tuple-element.243), channel_id=1, source_target_pairs={{0,16},{16,0},{1,17},{17,1},{2,18},{18,2},{3,19},{19,3},{4,20},{20... | collective-permute-start | bytes 1253384 | tf_op jit(solution)/shard_map/ppermute | solution.py:555
  293.4 28.5 %collective-permute-start.32 = (bf16[272,768]{1,0:T(8,128)(2,1)}, bf16[272,768]{1,0:T(8,128)(2,1)S(1)}, u32[]{:S(2)}, u32[]{:S(2)}) collective-permute-start(bf16[272,768]{1,0:T(8,128)(2,1)} %get-tuple-element.241), channel_id=1, source_target_pairs={{0,16},{16,0},{1,17},{17,1},{2,18},{18,2},{3,19},{19,3},{4,20},{20... | collective-permute-start | bytes 1253384 | tf_op jit(solution)/shard_map/ppermute | solution.py:555
  313.0 26.3 %collective-permute-start.31 = (bf16[272,768]{1,0:T(8,128)(2,1)S(1)}, bf16[272,768]{1,0:T(8,128)(2,1)S(1)}, u32[]{:S(2)}, u32[]{:S(2)}) collective-permute-start(bf16[272,768]{1,0:T(8,128)(2,1)S(1)} %copy-done.62), channel_id=1, source_target_pairs={{0,16},{16,0},{1,17},{17,1},{2,18},{18,2},{3,19},{19,3},{4,20},{20... | collective-permute-start | bytes 1253384 | tf_op jit(solution)/shard_map/ppermute | solution.py:555
  347.9 192.8 %reduce-scatter.3.cloned.1.call-start = ((), (), s32[]{:S(2)}) async-start(), calls=%async_computation.3 | async-start | bytes 3969024 | tf_op jit(solution)/shard_map/reduce_scatter | solution.py:1110
  419.0 76.7 %collective-permute-start.41 = (bf16[4,2,4,48,512]{4,3,2,1,0:T(8,128)(2,1)}, bf16[4,2,4,48,512]{4,3,2,1,0:T(8,128)(2,1)S(1)}, u32[]{:S(2)}, u32[]{:S(2)}) collective-permute-start(bf16[4,2,4,48,512]{4,3,2,1,0:T(8,128)(2,1)} %get-tuple-element.254), channel_id=1, source_target_pairs={{0,1},{1,0},{2,3},{3,2},{4,5},{5,4},{6,7},{7,6},{8,9},{9,8},{10,11... | collective-permute-start | bytes 4718600 | tf_op jit(solution)/shard_map/ppermute | solution.py:551
  425.9 69.9 %collective-permute-start.43 = (bf16[4,2,4,48,512]{4,3,2,1,0:T(8,128)(2,1)}, bf16[4,2,4,48,512]{4,3,2,1,0:T(8,128)(2,1)}, u32[]{:S(2)}, u32[]{:S(2)}) collective-permute-start(bf16[4,2,4,48,512]{4,3,2,1,0:T(8,128)(2,1)} %add_convert_fusion.1), channel_id=1, source_target_pairs={{0,2},{1,3},{2,0},{3,1},{4,6},{5,7},{6,4},{7,5},{8,10},{9,11},{10,... | collective-permute-start | bytes 4718600 | tf_op jit(solution)/shard_map/ppermute | solution.py:547
  427.5 64.5 %collective-permute-start.49 = (bf16[4,128,768]{2,1,0:T(8,128)(2,1)}, bf16[4,128,768]{2,1,0:T(8,128)(2,1)}, u32[]{:S(2)}, u32[]{:S(2)}) collective-permute-start(bf16[4,128,768]{2,1,0:T(8,128)(2,1)} %add_convert_fusion.3), channel_id=1, source_target_pairs={{0,2},{1,3},{2,0},{3,1},{4,6},{5,7},{6,4},{7,5},{8,10},{9,11},{10,... | collective-permute-start | bytes 2359304 | tf_op jit(solution)/shard_map/ppermute | solution.py:547
  500.7 28.2 %collective-permute-start.44 = (bf16[2,4,48,512]{3,2,1,0:T(8,128)(2,1)}, bf16[2,4,48,512]{3,2,1,0:T(8,128)(2,1)}, u32[]{:S(2)}, u32[]{:S(2)}) collective-permute-start(bf16[2,4,48,512]{3,2,1,0:T(8,128)(2,1)} %get-tuple-element.560), channel_id=1, source_target_pairs={{0,4},{1,5},{2,6},{3,7},{4,8},{5,9},{6,10},{7,11},{8,12},{9,13},{1... | collective-permute-start | bytes 1179656 | tf_op jit(solution)/shard_map/ppermute | solution.py:543
  502.2 33.4 %collective-permute-start.45 = (bf16[2,4,48,512]{3,2,1,0:T(8,128)(2,1)}, bf16[2,4,48,512]{3,2,1,0:T(8,128)(2,1)}, u32[]{:S(2)}, u32[]{:S(2)}) collective-permute-start(bf16[2,4,48,512]{3,2,1,0:T(8,128)(2,1)} %get-tuple-element.559), channel_id=1, source_target_pairs={{0,8},{1,9},{2,10},{3,11},{4,12},{5,13},{6,14},{7,15},{8,0},{9,1},... | collective-permute-start | bytes 1179656 | tf_op jit(solution)/shard_map/ppermute | solution.py:543
  505.0 33.9 %collective-permute-start.46 = (bf16[2,4,48,512]{3,2,1,0:T(8,128)(2,1)}, bf16[2,4,48,512]{3,2,1,0:T(8,128)(2,1)}, u32[]{:S(2)}, u32[]{:S(2)}) collective-permute-start(bf16[2,4,48,512]{3,2,1,0:T(8,128)(2,1)} %get-tuple-element.558), channel_id=1, source_target_pairs={{0,12},{1,13},{2,14},{3,15},{4,0},{5,1},{6,2},{7,3},{8,4},{9,5},{1... | collective-permute-start | bytes 1179656 | tf_op jit(solution)/shard_map/ppermute | solution.py:543
  (94 other events, 1195.1 us)
Sparse Core Ops, SparseCore 0:
  12.6 87.9 all-gather.1
  348.0 59.5 reduce-scatter.4
  411.5 79.4 reduce-scatter.2
